TPU v7x, 32 devices: a whole 2x2x4 slice. The times are simulated.
32 devices in a mesh: dp: 4 (over z), context: 4 (over y, core), tensor: 2 (over x).
Axes of the slice: x: 2, y: 2, z: 4, core: 2. Of those that a mesh axis runs over, the one named last changes fastest.
Arguments:
- hidden_in: bfloat16 [16, 2048, 768], P('dp', 'context'), may hold values from -6 to 6
- out_grad: bfloat16 [16, 2048, 768], P('dp', 'context'), may hold values from -6 to 6
- segment_ids: int32 [16, 2048], P('dp'), may hold values from 0 to 15, never falling along the last dimension, each value on 1 to 1024 neighbouring positions
- token_valid: int32 [16, 2048], P('dp'), may hold values 0 or 1
- random_blocks: int32 [16, 32, 3], P('dp'), may hold values from 2 to 31, as said below
- query_weight: bfloat16 [768, 768], P('dp', 'tensor'), may hold values from -0.21875 to 0.21875
- query_bias: bfloat16 [768], P('tensor'), may hold values from -3 to 3
- key_weight: bfloat16 [768, 768], P('dp', 'tensor'), may hold values from -0.21875 to 0.21875
- value_weight: bfloat16 [768, 768], P('dp', 'tensor'), may hold values from -0.21875 to 0.21875
- value_bias: bfloat16 [768], P('tensor'), may hold values from -3 to 3
- output_weight: bfloat16 [768, 768], P('tensor', 'dp'), may hold values from -0.625 to 0.625
- output_bias: bfloat16 [768], replicated, may hold values from -3 to 3
- norm1_gain: bfloat16 [768], replicated, may hold values from 0.5 to 1.5
- norm1_shift: bfloat16 [768], replicated, may hold values from -3 to 3
- up_weight: bfloat16 [768, 3072], P('dp', 'tensor'), may hold values from -0.21875 to 0.21875
- up_bias: bfloat16 [3072], P('tensor'), may hold values from -3 to 3
- down_weight: bfloat16 [3072, 768], P('tensor', 'dp'), may hold values from -0.109375 to 0.109375
- down_bias: bfloat16 [768], replicated, may hold values from -3 to 3
- norm2_gain: bfloat16 [768], replicated, may hold values from 0.5 to 1.5
- norm2_shift: bfloat16 [768], replicated, may hold values from -3 to 3
Outputs:
- layer_out: bfloat16 [16, 2048, 768], P('dp', 'context')
- input_grad: float32 [16, 2048, 768], P('dp', 'context')
- query_weight_grad: float32 [768, 768], P('dp', 'tensor')
- query_bias_grad: float32 [768], P('tensor')
- key_weight_grad: float32 [768, 768], P('dp', 'tensor')
- value_weight_grad: float32 [768, 768], P('dp', 'tensor')
- value_bias_grad: float32 [768], P('tensor')
- output_weight_grad: float32 [768, 768], P('tensor', 'dp')
- output_bias_grad: float32 [768], replicated
- norm1_gain_grad: float32 [768], replicated
- norm1_shift_grad: float32 [768], replicated
- up_weight_grad: float32 [768, 3072], P('dp', 'tensor')
- up_bias_grad: float32 [3072], P('tensor')
- down_weight_grad: float32 [3072, 768], P('tensor', 'dp')
- down_bias_grad: float32 [768], replicated
- norm2_gain_grad: float32 [768], replicated
- norm2_shift_grad: float32 [768], replicated
- input_rms: float32 [5], replicated
Inputs may be any that keep to these rules, and one draw needn't show every extreme that they name: `random_blocks`: for query block b the 3 numbers are distinct, none is 0, 1, b - 1, b or b + 1. `segment_ids`: numbers never fall along a sequence; a document spans 1 to 1024 tokens.
All inputs are finite; a program needn't handle non-finite values. No bound on the sum of `token_valid` on one device may be relied on, other than what follows from the above.
Results may differ from a plain program's by a relative error of at most 0.019.
Values may be sent and summed in bfloat16 or wider, within the bound.
A program may use at most 384 MiB of HBM per device.

v0:
```python
import functools

import jax
import jax.numpy as jnp
from jax import lax
from jax.experimental import pallas as pl
from jax.experimental.pallas import tpu as pltpu
from jax.sharding import PartitionSpec as P

HD = 64
BLK = 64
PAIR = 128
SLOTS = 8
WIDE = 512
SCALE = HD ** (-0.5)
EPSILON = 1e-06


NEG_FILL = -1e30
LEAP = 3
BACK_LEAP = 3


def pair_rows(block, left, scale=None):
    if scale is not None:
        block = block * jnp.asarray(scale, block.dtype)
    zero = jnp.zeros_like(block)
    return jnp.concatenate([jnp.where(left, block, zero), jnp.where(left, zero, block)], 0)


def lane_left(rows):
    return lax.broadcasted_iota(jnp.int32, (rows, PAIR), 1) < HD


def eye_pair():
    lanes = lax.broadcasted_iota(jnp.int32, (BLK, PAIR), 1)
    rows = lax.broadcasted_iota(jnp.int32, (BLK, PAIR), 0)
    return rows == lanes % BLK


def block_rows(index):
    return pl.ds(pl.multiple_of(index * BLK, BLK), BLK)


def slot_bias(slots, first_ok, third_ok, key_code, query_code, own):
    pieces = []
    for slot in range(SLOTS):
        code = query_code
        if slot == 0:
            code = jnp.where(first_ok, query_code, -2)
        if slot == 2:
            code = jnp.where(third_ok, query_code, -2)
        same = key_code[slots[slot]] == code
        if slot == 1:
            same = same | own
        pieces.append(jnp.where(same, 0.0, NEG_FILL))
    return jnp.concatenate(pieces, 0)


def slot_rows(ref, slots, lanes):
    return jnp.concatenate([ref[slot, :, lanes] for slot in slots], 0)


def wide_rows(ref, chunk, lanes):
    count = WIDE // BLK
    return ref[pl.ds(chunk * count, count), :, lanes].reshape(WIDE, PAIR)


def listed(table):
    def find(row):
        slots = [table[row, 1 + slot] for slot in range(SLOTS)]
        return table[row, 0], slots, table[row, 9] == 1, table[row, 10] == 1

    return find


def wide_bias(key_code, query_code, block, chunk):
    same = wide_rows(key_code, chunk, slice(0, PAIR)) == query_code
    key_pos = chunk * WIDE + lax.broadcasted_iota(jnp.int32, (WIDE, PAIR), 0)
    query_pos = block * BLK + lax.broadcasted_iota(jnp.int32, (WIDE, PAIR), 1) % BLK
    return jnp.where(same | (key_pos == query_pos), 0.0, NEG_FILL)


def dot_nt(left, right):
    return lax.dot_general(
        left, right, (((1,), (1,)), ((), ())), preferred_element_type=jnp.float32
    )


def dot_tn(left, right):
    return lax.dot_general(
        left, right, (((0,), (0,)), ((), ())), preferred_element_type=jnp.float32
    )


def dot_nn(left, right):
    return jnp.dot(left, right, preferred_element_type=jnp.float32)


def attend_kernel(table, wide, *refs):
    attend_blocks(listed(table), [wide[0], wide[1]], table.shape[0], [], *refs)


def attend_blocks(
    find, wide, count, marks, q_ref, k_ref, v_ref, key_code, query_code, o_ref, lse_ref, acc
):
    length, width = q_ref.shape
    pairs = width // PAIR
    left = lane_left(BLK)
    own = eye_pair()

    def narrow(row, carry):
        block, slots, first_ok, third_ok = find(row)
        rows = block_rows(block)
        code = query_code[pl.ds(block, 1), :]
        bias = slot_bias(slots, first_ok, third_ok, key_code, code, own)
        for pair in range(pairs):
            lanes = slice(pair * PAIR, (pair + 1) * PAIR)
            query = pair_rows(q_ref[rows, lanes], left, SCALE)
            scores = dot_nt(slot_rows(k_ref, slots, lanes), query) + bias
            top = jnp.max(scores, 0, keepdims=True)
            weight = jnp.exp(scores - top)
            total = jnp.sum(weight, 0, keepdims=True)
            probs = (weight * (1.0 / total)).astype(jnp.bfloat16)
            lse_ref[block, pl.ds(pair, 1), :] = top + jnp.log(total)
            both = dot_tn(probs, slot_rows(v_ref, slots, lanes))
            o_ref[rows, lanes] = jnp.where(left, both[:BLK], both[BLK:]).astype(o_ref.dtype)
        return carry

    leap = LEAP if count % LEAP == 0 else 1

    def stride(i, carry):
        for j in range(leap):
            narrow(i * leap + j, 0)
        for mark, action in marks:

            @pl.when(i == mark)
            def _():
                action()

        return carry

    lax.fori_loop(0, count // leap, stride, 0)

    def wide_step(which, nothing):
        block = wide[0] + which * (wide[1] - wide[0])
        rows = block_rows(block)
        code = query_code[pl.ds(block, 1), :]

        def first(chunk, carry):
            bias = wide_bias(key_code, code, block, chunk)
            out = []
            for pair in range(pairs):
                lanes = slice(pair * PAIR, (pair + 1) * PAIR)
                query = pair_rows(q_ref[rows, lanes], left, SCALE)
                scores = dot_nt(wide_rows(k_ref, chunk, lanes), query) + bias
                top_old, total_old = carry[pair]
                top = jnp.maximum(top_old, jnp.max(scores, 0, keepdims=True))
                total = total_old * jnp.exp(top_old - top) + jnp.sum(
                    jnp.exp(scores - top), 0, keepdims=True
                )
                out.append((top, total))
            return tuple(out)

        start = (jnp.full((1, PAIR), NEG_FILL), jnp.zeros((1, PAIR), jnp.float32))
        ends = lax.fori_loop(0, length // WIDE, first, (start,) * pairs, unroll=2)
        for pair in range(pairs):
            lse_ref[block, pl.ds(pair, 1), :] = ends[pair][0] + jnp.log(ends[pair][1])
        acc[...] = jnp.zeros_like(acc)

        def second(chunk, carry):
            bias = wide_bias(key_code, code, block, chunk)
            for pair in range(pairs):
                lanes = slice(pair * PAIR, (pair + 1) * PAIR)
                query = pair_rows(q_ref[rows, lanes], left, SCALE)
                scores = dot_nt(wide_rows(k_ref, chunk, lanes), query) + bias
                probs = jnp.exp(scores - lse_ref[block, pl.ds(pair, 1), :]).astype(jnp.bfloat16)
                acc[pair] += dot_tn(probs, wide_rows(v_ref, chunk, lanes))
            return carry

        lax.fori_loop(0, length // WIDE, second, 0, unroll=2)
        for pair in range(pairs):
            lanes = slice(pair * PAIR, (pair + 1) * PAIR)
            both = acc[pair]
            o_ref[rows, lanes] = jnp.where(left, both[:BLK], both[BLK:]).astype(o_ref.dtype)
        return nothing

    lax.fori_loop(0, 2, wide_step, 0)


def attend_back_kernel(table, wide, *refs):
    attend_back_blocks(listed(table), [wide[0], wide[1]], table.shape[0], *refs)


def attend_back_blocks(
    find, wide, count, q_ref, k_ref, v_ref, do_ref, key_code, query_code, lse_ref,
    dq_ref, dk_ref, dv_ref, dk_sum, dv_sum, dq_acc,
):
    length, width = q_ref.shape
    pairs = width // PAIR
    left = lane_left(BLK)
    own = eye_pair()
    dk_sum[...] = jnp.zeros_like(dk_sum)
    dv_sum[...] = jnp.zeros_like(dv_sum)

    def narrow(row, carry):
        block, slots, first_ok, third_ok = find(row)
        rows = block_rows(block)
        code = query_code[pl.ds(block, 1), :]
        bias = slot_bias(slots, first_ok, third_ok, key_code, code, own)
        for pair in range(pairs):
            lanes = slice(pair * PAIR, (pair + 1) * PAIR)
            query = pair_rows(q_ref[rows, lanes], left, SCALE)
            grad = pair_rows(do_ref[rows, lanes], left)
            keys = slot_rows(k_ref, slots, lanes)
            values = slot_rows(v_ref, slots, lanes)
            scores = dot_nt(keys, query) + bias
            probs = jnp.exp(scores - lse_ref[block, pl.ds(pair, 1), :])
            g_probs = dot_nt(values, grad)
            terms = probs * g_probs
            g_scores = (terms - probs * jnp.sum(terms, 0, keepdims=True)).astype(jnp.bfloat16)
            dv = dot_nn(probs.astype(jnp.bfloat16), grad)
            dk = dot_nn(g_scores, query)
            both = dot_tn(g_scores, keys)
            dq_ref[rows, lanes] = (jnp.where(left, both[:BLK], both[BLK:]) * SCALE).astype(
                dq_ref.dtype
            )
            for slot in range(SLOTS):
                spot = block_rows(slots[slot])
                part = slice(slot * BLK, (slot + 1) * BLK)
                dk_sum[spot, lanes] += dk[part]
                dv_sum[spot, lanes] += dv[part]
        return carry

    lax.fori_loop(0, count, narrow, 0, unroll=BACK_LEAP if count % BACK_LEAP == 0 else 1)

    def wide_step(which, nothing):
        block = wide[0] + which * (wide[1] - wide[0])
        rows = block_rows(block)
        code = query_code[pl.ds(block, 1), :]

        def pieces(chunk, pair, bias):
            keys_at = pl.ds(pl.multiple_of(chunk * WIDE, WIDE), WIDE)
            lanes = slice(pair * PAIR, (pair + 1) * PAIR)
            query = pair_rows(q_ref[rows, lanes], left, SCALE)
            grad = pair_rows(do_ref[rows, lanes], left)
            keys = wide_rows(k_ref, chunk, lanes)
            scores = dot_nt(keys, query) + bias
            probs = jnp.exp(scores - lse_ref[block, pl.ds(pair, 1), :])
            return keys_at, lanes, query, grad, keys, probs, probs * dot_nt(wide_rows(v_ref, chunk, lanes), grad)

        def first(chunk, carry):
            bias = wide_bias(key_code, code, block, chunk)
            return tuple(
                carry[pair] + jnp.sum(pieces(chunk, pair, bias)[-1], 0, keepdims=True)
                for pair in range(pairs)
            )

        deltas = lax.fori_loop(
            0, length // WIDE, first, (jnp.zeros((1, PAIR), jnp.float32),) * pairs
        )
        dq_acc[...] = jnp.zeros_like(dq_acc)

        def second(chunk, carry):
            bias = wide_bias(key_code, code, block, chunk)
            for pair in range(pairs):
                keys_at, lanes, query, grad, keys, probs, terms = pieces(chunk, pair, bias)
                g_scores = (terms - probs * carry[pair]).astype(jnp.bfloat16)
                dv_sum[keys_at, lanes] += dot_nn(probs.astype(jnp.bfloat16), grad)
                dk_sum[keys_at, lanes] += dot_nn(g_scores, query)
                dq_acc[pair] += dot_tn(g_scores, keys)
            return carry

        lax.fori_loop(0, length // WIDE, second, deltas)
        for pair in range(pairs):
            lanes = slice(pair * PAIR, (pair + 1) * PAIR)
            both = dq_acc[pair]
            dq_ref[rows, lanes] = (jnp.where(left, both[:BLK], both[BLK:]) * SCALE).astype(
                dq_ref.dtype
            )
        return nothing

    lax.fori_loop(0, 2, wide_step, 0)
    dk_ref[...] = dk_sum[...].astype(dk_ref.dtype)
    dv_ref[...] = dv_sum[...].astype(dv_ref.dtype)


def in_blocks(rows):
    return rows.reshape(-1, BLK, rows.shape[-1])


VMEM_SPEC = pl.BlockSpec(memory_space=pltpu.VMEM)
SMEM_SPEC = pl.BlockSpec(memory_space=pltpu.SMEM)
ROOM = pltpu.CompilerParams(vmem_limit_bytes=60 * 1024 * 1024)


def attend(table, wide, q, k, v, key_code, query_code):
    length, width = q.shape
    return pl.pallas_call(
        attend_kernel,
        out_shape=(
            jax.ShapeDtypeStruct((length, width), jnp.bfloat16),
            jax.ShapeDtypeStruct((length // BLK, 8, PAIR), jnp.float32),
        ),
        in_specs=[SMEM_SPEC] * 2 + [VMEM_SPEC] * 5,
        out_specs=(VMEM_SPEC, VMEM_SPEC),
        scratch_shapes=[pltpu.VMEM((width // PAIR, PAIR, PAIR), jnp.float32)],
        compiler_params=ROOM,
        cost_estimate=pl.CostEstimate(
            flops=length * width * 1024 * 60, bytes_accessed=length * width * 8,
            transcendentals=length * width * 8,
        ),
        name="attend",
    )(table, wide, q, in_blocks(k), in_blocks(v), in_blocks(key_code), query_code)


def attend_back(table, wide, q, k, v, do, key_code, query_code, lse):
    length, width = q.shape
    shape = jax.ShapeDtypeStruct((length, width), jnp.bfloat16)
    return pl.pallas_call(
        attend_back_kernel,
        out_shape=(shape, shape, shape),
        in_specs=[SMEM_SPEC] * 2 + [VMEM_SPEC] * 7,
        out_specs=(VMEM_SPEC,) * 3,
        scratch_shapes=[
            pltpu.VMEM((length, width), jnp.float32),
            pltpu.VMEM((length, width), jnp.float32),
            pltpu.VMEM((width // PAIR, PAIR, PAIR), jnp.float32),
        ],
        compiler_params=ROOM,
        cost_estimate=pl.CostEstimate(
            flops=length * width * 1024 * 70, bytes_accessed=length * width * 14,
            transcendentals=length * width * 8,
        ),
        name="attend_back",
    )(table, wide, q, in_blocks(k), in_blocks(v), do, in_blocks(key_code), query_code, lse)


GROUPS = 8
DUOS = GROUPS // 2
TILE = 256
FRONT = 512
ANY_SPEC = pl.BlockSpec(memory_space=pl.ANY)
DMA = pltpu.SemaphoreType.DMA
WIDE_ROOM = pltpu.CompilerParams(vmem_limit_bytes=63 * 1024 * 1024)


def normalize(values):
    row_mean = jnp.mean(values, -1, keepdims=True)
    centered = values - row_mean
    row_var = jnp.mean(centered * centered, -1, keepdims=True)
    inverse = lax.rsqrt(row_var + EPSILON)
    return centered * inverse, inverse


def normalize_back(grad, unit, inverse):
    return inverse * (
        grad
        - jnp.mean(grad, -1, keepdims=True)
        - unit * jnp.mean(grad * unit, -1, keepdims=True)
    )


def gelu_both(u):
    root = 0.7978845608028654
    square = u * u
    inner = jnp.tanh(u * (root + (root * 0.044715) * square))
    half = 0.5 + 0.5 * inner
    slope = half + u * (0.5 - 0.5 * (inner * inner)) * (root + (3.0 * root * 0.044715) * square)
    return u * half, slope


def start_copies(pairs, sem):
    copies = [pltpu.make_async_copy(src, dst, sem.at[i]) for i, (src, dst) in enumerate(pairs)]
    for copy in copies:
        copy.start()
    return copies


def wait_copies(copies):
    for copy in copies:
        copy.wait()


def row_of(ref):
    return ref[...].astype(jnp.float32).reshape(1, ref.shape[0])


def my_spot():
    place = lax.axis_index("context")
    return lax.axis_index("tensor"), place // 2, place % 2


def group_homes():
    half, turn, share = my_spot()
    return [
        ((half + h) % 2, ((turn + t) % 2) * 2 + (share + s) % 2)
        for s in range(2)
        for h in range(2)
        for t in range(2)
    ]


def lanes_of(g, cols):
    return pl.ds((g % 2) * cols, cols)


def place_block(block, per):
    half, turn, share = my_spot()
    chunk = block // per
    spot = ((share + chunk) % 2) * 2 + (turn + chunk // 2) % 2
    return spot * per + block % per


def computed(random, per, blocks):
    def find(row):
        block = row + 2
        ids = [block - 1, block, (block + 1) % blocks]
        slots = [place_block(i, per) for i in ids]
        slots += [place_block(jnp.int32(i), per) for i in range(2)]
        slots += [random[block * 3 + i] for i in range(3)]
        return slots[1], slots, block >= 3, block <= blocks - 2

    return find, [place_block(jnp.int32(i), per) for i in range(2)]


def write_codes(segments, live, key_code, query_code, span):
    half, turn, share = my_spot()
    row = pl.ds(half * 2 + turn, 1)
    left = lax.broadcasted_iota(jnp.int32, (1, PAIR), 1) < HD
    per = span // BLK
    for spot in range(4):
        chunk = ((turn + spot) % 2) * 2 + (share + spot // 2) % 2
        lanes = pl.ds(pl.multiple_of(chunk * span, span), span)
        seg = segments[row, lanes]
        code = jnp.where(live[row, lanes] == 1, seg, -1)
        key_code[pl.ds(spot * per, per)] = jnp.broadcast_to(code, (PAIR, span)).T.reshape(
            per, BLK, PAIR
        )
        for two in range(per // 2):
            both = seg[:, two * PAIR : (two + 1) * PAIR]
            turned = pltpu.roll(both, HD, 1)
            at = spot * per + 2 * two
            query_code[at : at + 1, :] = jnp.where(left, both, turned)
            query_code[at + 1 : at + 2, :] = jnp.where(left, turned, both)


def project_attend_kernel(
    random, hidden, x_in, q_all, f_deep, n1_in, n2_in, segments, live, b_q, b_v, far_q, far_v,
    own_ref, other_home, q_home, k_home, v_home, w_home,
    n1, n2, n3, f0, f1, f2, f3, lse_ref, key_code, query_code,
    x_v, q_v, k_v, v_v, o_v, w_v, acc, in_sem, out_sem, w_sem, send_sem, recv_sem,
):
    span = hidden.shape[1]
    length, width = q_v.shape
    depth = f_deep.shape[0]
    half, turn, share = my_spot()
    across, beside, partner = neighbours()
    weights = start_copies(
        [(q_all.at[share, t, s], w_v.at[:, t, s]) for t in range(2) for s in range(2)], w_sem
    )
    chunks = [hidden.at[half * 2 + turn]] + [x_in.at[i] for i in range(3)]
    loads = start_copies(
        [(x, x_v.at[pl.ds(i * span, span)]) for i, x in enumerate(chunks)], in_sem
    )
    deep = lax.axis_index("dp")
    deeps = [{"dp": (deep + j) % depth} for j in range(1, depth)]
    signal_all([across, beside, partner] + deeps)
    ids = iter(range(send_sem.shape[0]))
    started = []

    def link(src, dst, device):
        i = next(ids)
        started.append(remote(src, dst, send_sem.at[i], recv_sem.at[i], device))
        return started[-1]

    at = [(deep + j) % depth for j in range(depth)]
    rest_of = range(1, depth)
    corner = [link(n2.at[at[j]], n3.at[at[j]], beside) for j in range(depth)]
    to_across = {j: link(f_deep.at[at[j]], n2.at[at[j]], across) for j in rest_of}
    along = {depth - j: link(n1.at[deep], n1.at[deep], deeps[j - 1]) for j in rest_of}
    ends = [
        [link(home.at[at[j]], landing.at[at[j]], partner) for j in range(depth)]
        for home, landing in ((f_deep, f0), (n1, f1), (n2, f2), (n3, f3))
    ]
    swap = link(o_v.at[pl.ds(length // 2, length // 2)], other_home, partner)
    corner[0].start()
    for j in rest_of:
        to_across[j].start()
        along[depth - j].start()
    for copy in ends[0] + [ends[1][0], ends[2][0]]:
        copy.start()

    def from_side(j):
        along[j].wait_recv()
        ends[1][j].start()

    def from_far(j):
        to_across[j].wait_recv()
        ends[2][j].start()
        corner[j].start()

    def from_corner(j):
        corner[j].wait_recv()
        ends[3][j].start()

    steps = [[(from_far, j)] for j in rest_of]
    steps[0].append((from_corner, 0))
    steps += [[(from_side, j) for j in rest_of] + [(from_corner, 1)]]
    steps += [[(from_corner, j)] for j in range(2, depth)]

    def take_step(index):
        for action, j in steps[index]:
            action(j)

    write_codes(segments, live, key_code, query_code, span)
    same = half == share
    bias = jnp.concatenate(
        [
            jnp.where(same, row_of(b_q), row_of(far_q)),
            jnp.zeros((1, width), jnp.float32),
            jnp.where(same, row_of(b_v), row_of(far_v)),
        ],
        1,
    )
    wait_copies(weights)
    wait_copies(loads)
    per = span // BLK

    def project(i, carry):
        at = pl.ds(pl.multiple_of(i * span, span), span)
        w_qkv = w_v[...].reshape(x_v.shape[1], 3 * width)
        value = (dot_nn(x_v[at, :], w_qkv) + bias).astype(jnp.bfloat16)
        q_v[at, :] = value[:, :width]
        k_v[pl.ds(i * per, per)] = value[:, width : 2 * width].reshape(per, BLK, width)
        v_v[pl.ds(i * per, per)] = value[:, 2 * width :].reshape(per, BLK, width)
        return carry

    lax.fori_loop(0, 4, project, 0)
    stores = start_copies([(q_v, q_home), (k_v, k_home), (v_v, v_home), (w_v, w_home)], out_sem)
    blocks = length // BLK
    find, wide = computed(random, span // BLK, blocks)
    count = blocks - 2
    early = min(5, count // LEAP // 2, len(steps))
    marks = [(2 * i + 1, functools.partial(take_step, i)) for i in range(early)]
    attend_blocks(
        find, wide, count, marks, q_v, k_v, v_v, key_code, query_code, o_v, lse_ref, acc
    )
    own_ref[...] = o_v[: length // 2, :]
    swap.start()
    for index in range(early, len(steps)):
        take_step(index)
    for copy in ends[0] + ends[1] + ends[2] + ends[3] + [swap]:
        copy.wait_recv()
    for copy in started:
        copy.wait_send()
    wait_copies(stores)


def project_attend(
    random, hidden, x_in, q_all, f_deep, n1, n2, segments, live, b_q, b_v, far_q, far_v
):
    span, features = hidden.shape[1:]
    length = 4 * span
    depth, slim, cols = q_all.shape[3:]
    width = cols // 3
    bf16, shape = jnp.bfloat16, jax.ShapeDtypeStruct
    piece = shape(f_deep.shape, bf16)
    outs = pl.pallas_call(
        project_attend_kernel,
        out_shape=(shape((length // 2, width), bf16),) * 2
        + (shape((length, width), bf16),)
        + (shape((length // BLK, BLK, width), bf16),) * 2
        + (shape((depth, 2, 2, slim, cols), bf16),)
        + (piece,) * 7
        + (
            shape((length // BLK, 8, PAIR), jnp.float32),
            shape((length // BLK, BLK, PAIR), jnp.int32),
            shape((length // BLK, PAIR), jnp.int32),
        ),
        in_specs=[SMEM_SPEC] + [ANY_SPEC] * 6 + [VMEM_SPEC] * 6,
        out_specs=(VMEM_SPEC,) + (ANY_SPEC,) * 12 + (VMEM_SPEC,) * 3,
        scratch_shapes=[pltpu.VMEM((length, features), bf16)]
        + [pltpu.VMEM((length, width), bf16)]
        + [pltpu.VMEM((length // BLK, BLK, width), bf16)] * 2
        + [pltpu.VMEM((length, width), bf16)]
        + [
            pltpu.VMEM((depth, 2, 2, slim, cols), bf16),
            pltpu.VMEM((width // PAIR, PAIR, PAIR), jnp.float32),
            DMA((4,)), DMA((4,)), DMA((4,)), DMA((8 * depth + 2,)), DMA((8 * depth + 2,)),
        ],
        input_output_aliases={5: 6, 6: 7},
        compiler_params=pltpu.CompilerParams(
            vmem_limit_bytes=63 * 1024 * 1024, collective_id=3, has_side_effects=True
        ),
        cost_estimate=pl.CostEstimate(
            flops=length * width * 1024 * 65, bytes_accessed=length * width * 16,
            transcendentals=length * width * 8,
        ),
        name="project_attend",
    )(
        random, hidden, x_in, q_all, f_deep, n1, n2, segments, live, b_q, b_v, far_q, far_v
    )
    att0, att1, q, k, v, w_qkv, *pieces, lse, key_code, query_code = outs
    w_qkv = w_qkv.reshape(features, cols)
    return att0, att1, q, k, v, lse, w_qkv, [f_deep] + pieces, key_code, query_code


def attend_grad_kernel(
    random, do0, do1, q_in, k_in, v_in, layer, key_code, query_code, lse_ref,
    d_ref, layer_home, sums,
    layer_v, layer_sem, q_v, k_v, v_v, do_v, dk_sum, dv_sum, acc, in_sem,
):
    f32 = jnp.float32
    length, width = q_v.shape
    half_length = length // 2
    loads = start_copies(
        [
            (q_in, q_v), (k_in, k_v), (v_in, v_v),
            (do0, do_v.at[pl.ds(0, half_length)]),
            (do1, do_v.at[pl.ds(half_length, half_length)]),
        ],
        in_sem,
    )
    take = pltpu.make_async_copy(layer, layer_v, layer_sem.at[0])
    put = pltpu.make_async_copy(layer_v, layer_home, layer_sem.at[1])
    take.start()
    wait_copies(loads)
    take.wait()
    put.start()
    parts = [d_ref.at[:, pl.ds(i * width, width)] for i in range(3)]
    blocks = length // BLK
    find, wide = computed(random, blocks // 4, blocks)
    attend_back_blocks(
        find, wide, blocks - 2, q_v, k_v, v_v, do_v, key_code, query_code, lse_ref,
        *parts, dk_sum, dv_sum, acc,
    )
    share = my_spot()[2]
    sums[...] = jnp.zeros_like(sums)
    for s in range(2):

        @pl.when(share == s)
        def _():
            lanes = slice(s * width, (s + 1) * width)
            sums[0:1, lanes] = jnp.sum(d_ref[:, :width].astype(f32), 0, keepdims=True)
            sums[1:2, lanes] = jnp.sum(d_ref[:, 2 * width :].astype(f32), 0, keepdims=True)
    put.wait()


def attend_grad(random, do0, do1, q, k, v, layer, key_code, query_code, lse):
    length, width = q.shape
    f32, bf16, shape = jnp.float32, jnp.bfloat16, jax.ShapeDtypeStruct
    return pl.pallas_call(
        attend_grad_kernel,
        out_shape=(
            shape((length, 3 * width), bf16), shape(layer.shape, bf16), shape((8, 2 * width), f32)
        ),
        in_specs=[SMEM_SPEC] + [ANY_SPEC] * 6 + [VMEM_SPEC] * 3,
        out_specs=(VMEM_SPEC, ANY_SPEC, VMEM_SPEC),
        scratch_shapes=[pltpu.VMEM(layer.shape, bf16), DMA((2,))]
        + [pltpu.VMEM((length, width), bf16)]
        + [pltpu.VMEM((length // BLK, BLK, width), bf16)] * 2
        + [pltpu.VMEM((length, width), bf16)]
        + [pltpu.VMEM((length, width), f32)] * 2
        + [pltpu.VMEM((width // PAIR, PAIR, PAIR), f32), DMA((5,))],
        compiler_params=WIDE_ROOM,
        cost_estimate=pl.CostEstimate(
            flops=length * width * 1024 * 75, bytes_accessed=length * width * 30,
            transcendentals=length * width * 8,
        ),
        name="attend_grad",
    )(random, do0, do1, q, k, v, layer, key_code, query_code, lse)


def load_weights(groups, w_up, w_dn, w_out, up_sem, dn_sem, wo_sem):
    depth, deep, cols = groups[0].shape
    thin = w_up.shape[2]
    slim = deep - 2 * thin
    homes = group_homes()
    out_loads = []
    for g in range(GROUPS):
        half, at = homes[g]
        for d in range(depth):
            spot = pl.ds(pl.multiple_of(d * thin + at * slim, 16), slim)
            out_loads.append(
                pltpu.make_async_copy(
                    groups[g].at[d, pl.ds(2 * thin, slim)], w_out.at[half, spot], wo_sem.at[g, d]
                )
            )
    up_loads = [
        pltpu.make_async_copy(
            groups[g].at[:, pl.ds(0, thin)], w_up.at[g // 2, :, :, lanes_of(g, cols)], up_sem.at[g]
        )
        for g in range(GROUPS)
    ]
    dn_loads = [
        pltpu.make_async_copy(
            groups[g].at[:, pl.ds(thin, thin)],
            w_dn.at[g // 2, :, :, lanes_of(g, cols)],
            dn_sem.at[g],
        )
        for g in range(GROUPS)
    ]
    return out_loads, up_loads, dn_loads


def whole(ref, g):
    depth, thin, cols = ref.shape[1:]
    return ref[g].reshape(depth * thin, cols)


def ffn_front_kernel(att0, att1, hidden, x_in, g_all, *rest):
    groups = rest[:GROUPS]
    (
        key_code, v_out, v_gain1, v_shift1, v_down, v_gain2, v_shift2, b_near, b_far,
        out0_home, out1_home, slope_home, g_second_home, unit_home, norm_t_home, down_home,
        inverse_ref, sums,
        att_v, x_v, g_v, w_up, w_dn, w_out, act, slope, normed_low,
        out_v, g_second_v, unit_v, norm_t, g_ffn_t, stage, b_up, b_all,
        in_sem, up_sem, dn_sem, wo_sem, stage_sem, home_sem, end_sem, g_sem,
    ) = rest[GROUPS:]
    f32, bf16 = jnp.float32, jnp.bfloat16
    rows, width = x_v.shape
    span = hidden.shape[1]
    depth, deep, cols = groups[0].shape
    half, turn, share = my_spot()
    x_chunks = (hidden.at[half * 2 + turn], x_in.at[0])
    g_chunks = (g_all.at[half * 2 + turn],)
    other = (share + 1) % 2
    out_loads, up_loads, dn_loads = load_weights(groups, w_up, w_dn, w_out, up_sem, dn_sem, wo_sem)
    loads = start_copies(
        [(a, att_v.at[:, lanes_of(i, cols)]) for i, a in enumerate((att0, att1))]
        + [(x, x_v.at[pl.ds(i * span, span)]) for i, x in enumerate(x_chunks)]
        + [(g, g_v.at[pl.ds(i * span, span)]) for i, g in enumerate(g_chunks)],
        in_sem,
    )
    for copy in out_loads + up_loads + dn_loads:
        copy.start()
    beside = neighbours()[1]
    signal_all([beside])
    g_next = remote(
        g_all.at[half * 2 + (turn + 1) % 2], g_v.at[pl.ds(span, span)], g_sem.at[0], g_sem.at[1],
        beside,
    )
    g_next.start()
    sums[...] = jnp.zeros_like(sums)
    b_all[0:1, :] = row_of(b_near)
    b_all[1:2, :] = row_of(b_far)
    for g in range(GROUPS):
        at = group_homes()[g][1]
        lanes = pl.ds(pl.multiple_of(at * cols, PAIR), cols)
        value = b_all[g // 2 % 2 : g // 2 % 2 + 1, lanes]
        b_up[g // 2 : g // 2 + 1, (g % 2) * cols : (g % 2 + 1) * cols] = value
    wait_copies(loads + out_loads)
    b_out, gain1, shift1, b_down, gain2, shift2 = (
        row_of(ref) for ref in (v_out, v_gain1, v_shift1, v_down, v_gain2, v_shift2)
    )

    def add_sum(index, value):
        sums[index : index + 1, :] += jnp.sum(value, 0, keepdims=True)

    def homes(tile):
        at = pl.ds(pl.multiple_of(tile * FRONT, FRONT), FRONT)
        return [
            pltpu.make_async_copy(src, dst, home_sem.at[i, tile])
            for i, (src, dst) in enumerate(
                [
                    (slope.at[:, at], slope_home.at[:, at]),
                    (g_second_v.at[at], g_second_home.at[at]),
                    (unit_v.at[at], unit_home.at[at]),
                ]
            )
        ]

    def tile_step(tile, carry):
        at = pl.ds(pl.multiple_of(tile * FRONT, FRONT), FRONT)
        live = (key_code[at, :1] >= 0).astype(f32)
        add_sum(11, jnp.broadcast_to(live, (FRONT, width)))
        attn = b_out + dot_nt(att_v[at, :], jnp.concatenate([w_out[share], w_out[other]], 1))
        x = x_v[at, :].astype(f32)
        first = x + attn
        add_sum(6, live * (x * x))
        add_sum(7, live * (first * first))
        add_sum(9, live * (attn * attn))
        unit1, inverse1 = normalize(first)
        unit_v[at, :] = unit1
        inverse_ref[at, :] = inverse1
        normed = unit1 * gain1 + shift1
        low = normed.astype(bf16)
        normed_low[...] = low
        norm_t[:, at] = low.T

        @pl.when(tile == 0)
        def _():
            wait_copies(up_loads + dn_loads)

        @pl.when(tile == span // FRONT)
        def _():
            g_next.wait_recv()

        def up_step(g, ffn):
            pre = dot_nn(normed_low[...], whole(w_up, g)) + b_up[pl.ds(g, 1), :]
            value, rise = gelu_both(pre)
            value = value.astype(bf16)
            act[g, at, :] = value
            slope[g, at, :] = rise.astype(bf16)
            return ffn + dot_nt(value, whole(w_dn, g))

        ffn = lax.fori_loop(0, DUOS, up_step, jnp.broadcast_to(b_down, (FRONT, width)))
        second = normed + ffn
        add_sum(8, live * (second * second))
        add_sum(10, live * (ffn * ffn))
        unit2, inverse2 = normalize(second)
        out_v[at, :] = (unit2 * gain2 + shift2).astype(bf16)
        g_out = g_v[at, :].astype(f32)
        add_sum(4, g_out * unit2)
        add_sum(5, g_out)
        g_second = normalize_back(g_out * gain2, unit2, inverse2)
        g_second_v[at, :] = g_second
        g_ffn = g_second.astype(bf16)
        add_sum(3, g_ffn.astype(f32))
        g_ffn_t[:, at] = g_ffn.T
        for copy in homes(tile):
            copy.start()
        return carry

    lax.fori_loop(0, rows // FRONT, tile_step, 0)
    last = start_copies(
        [
            (norm_t, norm_t_home),
            (out_v.at[pl.ds(0, span)], out0_home),
            (out_v.at[pl.ds(span, span)], out1_home),
        ],
        end_sem,
    )

    def leave(g):
        return pltpu.make_async_copy(stage.at[g], down_home.at[g], stage_sem.at[g])

    def down_step(duo, carry):
        down = dot_nn(g_ffn_t[...], act[duo]).astype(bf16).reshape(depth, -1, 2 * cols)
        for i in range(2):
            stage[2 * duo + i] = down[:, :, i * cols : (i + 1) * cols]
            leave(2 * duo + i).start()
        return carry

    lax.fori_loop(0, DUOS, down_step, 0)
    for tile in range(rows // FRONT):
        wait_copies(homes(tile))
    wait_copies([leave(g) for g in range(GROUPS)] + last)
    g_next.wait_send()


def ffn_front(att0, att1, hidden, x_in, g_all, groups, key_code, vectors, b_near, b_far):
    rows, part = att0.shape
    width = hidden.shape[2]
    depth, deep, cols = groups[0].shape
    thin = width // depth
    f32, bf16, shape = jnp.float32, jnp.bfloat16, jax.ShapeDtypeStruct
    weights = pltpu.VMEM((DUOS, depth, thin, 2 * cols), bf16)
    flat = pltpu.VMEM((rows, width), bf16)
    tall = pltpu.VMEM((rows, width), f32)
    deep_rows = pltpu.VMEM((DUOS, rows, 2 * cols), bf16)
    turned = pltpu.VMEM((width, rows), bf16)
    return pl.pallas_call(
        ffn_front_kernel,
        out_shape=(
            shape((rows // 2, width), bf16), shape((rows // 2, width), bf16),
            shape((DUOS, rows, 2 * cols), bf16),
            shape((rows, width), f32), shape((rows, width), f32), shape((width, rows), bf16),
            shape((GROUPS, depth, thin, cols), bf16), shape((rows, 1), f32), shape((16, width), f32),
        ),
        in_specs=[ANY_SPEC] * (5 + GROUPS) + [VMEM_SPEC] * 9,
        out_specs=(ANY_SPEC,) * 7 + (VMEM_SPEC,) * 2,
        scratch_shapes=[
            flat, flat, flat, weights, weights, pltpu.VMEM((2, width, part), bf16),
            deep_rows, deep_rows, pltpu.VMEM((FRONT, width), bf16),
            flat, tall, tall, turned, turned, pltpu.VMEM((GROUPS, depth, thin, cols), bf16),
            pltpu.VMEM((DUOS, 2 * cols), f32), pltpu.VMEM((2, 4 * cols), f32),
            DMA((6,)), DMA((GROUPS,)), DMA((GROUPS,)), DMA((GROUPS, depth)), DMA((GROUPS,)),
            DMA((3, rows // FRONT)), DMA((3,)), DMA((2,)),
        ],
        compiler_params=pltpu.CompilerParams(
            vmem_limit_bytes=63 * 1024 * 1024, collective_id=4, has_side_effects=True
        ),
        cost_estimate=pl.CostEstimate(
            flops=38 * 10**9, bytes_accessed=40 * 10**6, transcendentals=rows * GROUPS * cols
        ),
        name="ffn_front",
    )(att0, att1, hidden, x_in, g_all, *groups, key_code, *vectors, b_near, b_far)


def ffn_rear_kernel(
    att0, att1, slope_in, g_second_in, unit_in, norm_t_in, out0, out1, downs, *rest
):
    groups = rest[:GROUPS]
    (
        inverse_ref, v_gain1,
        g_first_home, do_own, do_far, layer_home, *totals
    ) = rest[GROUPS : GROUPS + 5 + DUOS + groups[0].shape[0]]
    corners = totals[DUOS - 1 :]
    (
        sums, up_sums,
        att_v, slope, g_second_v, unit_v, norm_t, w_up, w_dn, w_out, g_pre,
        g_first_v, g_att_v, g_attn_t, out_v, far_v, got_v, got_dn, near_v, stage,
        in_sem, up_sem, dn_sem, wo_sem, stage_sem, home_sem, out_sem,
        l_send, l_recv, a_send, a_recv, u_send, u_recv, corner_sem,
    ) = rest[GROUPS + 5 + DUOS + len(corners) :]
    f32, bf16 = jnp.float32, jnp.bfloat16
    rows, width = unit_v.shape
    span = out0.shape[0]
    depth, deep, cols = groups[0].shape
    thin = w_up.shape[2]
    slim = deep - 2 * thin
    half, turn, share = my_spot()
    other = (share + 1) % 2
    across, beside, partner = neighbours()
    out_loads, up_loads, dn_loads = load_weights(groups, w_up, w_dn, w_out, up_sem, dn_sem, wo_sem)
    wait_order = [
        pltpu.make_async_copy(src, dst, in_sem.at[i])
        for i, (src, dst) in enumerate(
            [
                (g_second_in, g_second_v), (slope_in, slope), (unit_in, unit_v),
                (norm_t_in, norm_t), (att0, att_v.at[:, lanes_of(0, cols)]),
                (att1, att_v.at[:, lanes_of(1, cols)]),
            ]
        )
    ]
    for copy in wait_order[:1] + dn_loads + wait_order[1:2] + up_loads + wait_order[2:3]:
        copy.start()
    for copy in out_loads + wait_order[3:]:
        copy.start()
    late = start_copies([(out0, out_v), (downs.at[pl.ds(0, DUOS)], near_v)], out_sem)
    signal_all([across, beside, partner])
    mine = layer_home.at[half * 2 + turn]
    theirs = layer_home.at[half * 2 + (turn + 1) % 2]
    parts = [pl.ds(i * (span // 2), span // 2) for i in range(2)]
    layer = [
        remote(out1.at[parts[0]], mine.at[parts[0]], l_send.at[0], l_recv.at[0], beside),
        remote(out0, mine, l_send.at[1], l_recv.at[1], across),
        remote(theirs.at[parts[0]], theirs.at[parts[0]], l_send.at[2], l_recv.at[2], across),
        remote(downs.at[pl.ds(DUOS, DUOS)], got_dn, l_send.at[3], l_recv.at[3], partner),
        remote(out1.at[parts[1]], mine.at[parts[1]], l_send.at[4], l_recv.at[4], beside),
        remote(theirs.at[parts[1]], theirs.at[parts[1]], l_send.at[5], l_recv.at[5], across),
    ]
    for i in (0, 4, 1, 3):
        layer[i].start()
    sums[...] = jnp.zeros_like(sums)
    up_sums[...] = jnp.zeros_like(up_sums)
    gain1 = row_of(v_gain1)
    wait_copies(wait_order[:1] + dn_loads + wait_order[1:2])
    out_weight = lambda: jnp.concatenate([w_out[share], w_out[other]], 1)

    def add_sum(index, value):
        sums[index : index + 1, :] += jnp.sum(value, 0, keepdims=True)

    def tile_rows(tile):
        return pl.ds(pl.multiple_of(tile * TILE, TILE), TILE)

    def give(tile):
        at = tile_rows(tile)
        return remote(g_att_v.at[1, at], do_far.at[at], a_send.at[tile], a_recv.at[tile], partner)

    tiles = rows // TILE

    def tile_step(tile, carry):
        at = tile_rows(tile)

        @pl.when(tile == 0)
        def _():
            wait_copies(up_loads + wait_order[2:] + out_loads)

        for late_tile, i in ((tiles - 2, 0), (tiles - 1, 1)):

            @pl.when(tile == late_tile)
            def _():
                layer[(0, 4)[i]].wait_recv()
                layer[(2, 5)[i]].start()

        g_second = g_second_v[at, :]
        g_ffn = g_second.astype(bf16)

        def back_step(g, total):
            grad = (dot_nn(g_ffn, whole(w_dn, g)) * slope[g, at, :].astype(f32)).astype(bf16)
            g_pre[g, at, :] = grad
            up_sums[pl.ds(g, 1), :] += jnp.sum(grad.astype(f32), 0, keepdims=True)
            return total + dot_nt(grad, whole(w_up, g))

        g_normed = lax.fori_loop(0, DUOS, back_step, g_second)
        unit1 = unit_v[at, :]
        add_sum(1, g_normed * unit1)
        add_sum(2, g_normed)
        g_first = normalize_back(g_normed * gain1, unit1, inverse_ref[at, :])
        g_first_v[at, :] = g_first
        g_attn = g_first.astype(bf16)
        add_sum(0, g_attn.astype(f32))
        g_attn_t[:, at] = g_attn.T
        both = dot_nn(g_attn, out_weight()).astype(bf16)
        g_att_v[0, at, :] = both[:, :cols]
        g_att_v[1, at, :] = both[:, cols:]
        give(tile).start()
        return carry

    lax.fori_loop(0, tiles, tile_step, 0)
    homes = start_copies([(g_att_v.at[0], do_own), (g_first_v, g_first_home)], home_sem)
    wait_copies(late)
    own_out = pltpu.make_async_copy(out_v, mine, out_sem.at[0])
    own_out.start()
    both = dot_nn(g_attn_t[...], att_v[...]).astype(bf16)
    w_out[share] = both[:, :cols]
    w_out[other] = both[:, cols:]

    def out_rows(g, d):
        where = (half + g // 2) % 2
        at = ((turn + g) % 2) * 2 + (share + g // 4) % 2
        return w_out[where, pl.ds(pl.multiple_of(d * thin + at * slim, 16), slim), :]

    def up_of(duo):
        up = dot_nn(norm_t[...], g_pre[duo]).astype(bf16).reshape(depth, thin, 2 * cols)
        return [(2 * duo + i, up[:, :, i * cols : (i + 1) * cols]) for i in range(2)]

    def pass_on(i):
        return remote(far_v.at[i], got_v.at[i], u_send.at[i], u_recv.at[i], partner)

    def far_step(duo, carry):
        for g, up in up_of(duo):
            i = g - DUOS
            far_v[i, :, pl.ds(0, thin), :] = up
            for d in range(depth):
                far_v[i, d, pl.ds(thin, slim), :] = out_rows(g, d)
            pass_on(i).start()
        return carry

    lax.fori_loop(DUOS // 2, DUOS, far_step, 0)
    sends = [pass_on(i) for i in range(DUOS)]
    layer[3].wait_recv()
    add = lambda a, b: (a.astype(f32) + b.astype(f32)).astype(bf16)
    stores = [None] * DUOS
    for duo in range(DUOS // 2):
        for g, up in up_of(duo):
            slot = g % 2
            if g >= 2:
                stores[g - 2].wait()
            sends[g].wait_recv()
            stage[slot, :, pl.ds(0, thin), :] = add(up, got_v[g, :, pl.ds(0, thin), :])
            stage[slot, :, pl.ds(thin, thin), :] = add(near_v[g], got_dn[g])
            for d in range(depth):
                stage[slot, d, pl.ds(2 * thin, slim), :] = add(
                    out_rows(g, d), got_v[g, d, pl.ds(thin, slim), :]
                )
            if g == DUOS - 1:
                deep_at = lax.axis_index("dp")
                rounds = start_copies(
                    [
                        (stage.at[slot, (deep_at + j) % depth], home)
                        for j, home in enumerate(corners)
                    ],
                    corner_sem,
                )
                continue
            stores[g] = pltpu.make_async_copy(stage.at[slot], totals[g], stage_sem.at[slot])
            stores[g].start()
    for tile in range(tiles):
        give(tile).wait()
    for i in (1, 2, 5):
        layer[i].wait_recv()
    for copy in layer + sends:
        copy.wait_send()
    wait_copies(stores[-2:-1] + rounds + homes + [own_out])


def ffn_rear(
    att0, att1, slope, g_second, unit, norm_t, out0, out1, downs_in, groups, inverse, gain1
):
    rows, part = att0.shape
    span, width = out0.shape
    depth, deep, cols = groups[0].shape
    thin = width // depth
    f32, bf16, shape, v = jnp.float32, jnp.bfloat16, jax.ShapeDtypeStruct, pltpu.VMEM
    weights = v((DUOS, depth, thin, 2 * cols), bf16)
    flat = v((rows, width), bf16)
    tall = v((rows, width), f32)
    deep_rows = v((DUOS, rows, 2 * cols), bf16)
    turned = v((width, rows), bf16)
    mixed = v((DUOS, depth, deep - thin, cols), bf16)
    downs = v((DUOS, depth, thin, cols), bf16)
    tiles = rows // TILE
    return pl.pallas_call(
        ffn_rear_kernel,
        out_shape=(
            shape((rows, width), f32), shape((rows, part), bf16), shape((rows, part), bf16),
            shape((4, span, width), bf16),
        )
        + (shape((depth, deep, cols), bf16),) * (DUOS - 1)
        + (shape((deep, cols), bf16),) * depth
        + (shape((16, width), f32), shape((DUOS, 2 * cols), f32)),
        in_specs=[ANY_SPEC] * (9 + GROUPS) + [VMEM_SPEC] * 2,
        out_specs=(ANY_SPEC,) * (3 + DUOS + depth) + (VMEM_SPEC,) * 2,
        scratch_shapes=[
            flat, deep_rows, tall, tall, turned, weights, weights,
            v((2, width, part), bf16), deep_rows, tall, v((2, rows, part), bf16), turned,
            v((span, width), bf16), mixed, mixed, downs, downs, v((2, depth, deep, cols), bf16),
            DMA((6,)), DMA((GROUPS,)), DMA((GROUPS,)), DMA((GROUPS, depth)), DMA((2,)), DMA((2,)),
            DMA((2,)), DMA((6,)), DMA((6,)), DMA((tiles,)), DMA((tiles,)), DMA((DUOS,)),
            DMA((DUOS,)), DMA((depth,)),
        ],
        compiler_params=pltpu.CompilerParams(
            vmem_limit_bytes=63 * 1024 * 1024, collective_id=2, has_side_effects=True
        ),
        cost_estimate=pl.CostEstimate(
            flops=45 * 10**9, bytes_accessed=40 * 10**6, transcendentals=0
        ),
        name="ffn_rear",
    )(
        att0, att1, slope, g_second, unit, norm_t, out0, out1, downs_in, *groups, inverse, gain1
    )


MESH = pl.DeviceIdType.MESH
CUTS = 8
THIRDS = 3


def signal_all(devices):
    barrier = pltpu.get_barrier_semaphore()
    for device in devices:
        pl.semaphore_signal(barrier, inc=1, device_id=device, device_id_type=MESH)
    pl.semaphore_wait(barrier, len(devices))


def neighbours():
    half, turn, share = my_spot()
    return (
        {"tensor": (half + 1) % 2},
        {"context": ((turn + 1) % 2) * 2 + share},
        {"context": turn * 2 + (share + 1) % 2},
    )


def remote(src, dst, send_sem, recv_sem, device):
    return pltpu.make_async_remote_copy(
        src_ref=src, dst_ref=dst, send_sem=send_sem, recv_sem=recv_sem,
        device_id=device, device_id_type=MESH,
    )


def fetch_kernel(
    hidden, w_q, w_k, w_v, w_up, w_down, w_out, bias_q, bias_v, bias_u,
    x_out, q_all, f_deep, n1, n2, far_q, far_v, far_u,
    qkv, ffn, cut_sem, own_sem, x_send, x_recv, z_send, z_recv, f_send, f_recv,
    h_send, h_recv, t_send, t_recv, c_send, c_recv, b_sem, n_send, n_recv,
):
    half, turn, share = my_spot()
    deep = lax.axis_index("dp")
    depth = f_deep.shape[0]
    across, beside, partner = neighbours()
    up, down = {"dp": (deep + 1) % depth}, {"dp": (deep + depth - 1) % depth}
    slim, thin, cols = qkv.shape[0], w_q.shape[0], w_q.shape[1]
    place = turn * 2 + share
    my_rows = pl.ds(pl.multiple_of(place * slim, 16), slim)
    my_lanes = pl.ds(pl.multiple_of(place * cols, PAIR), cols)
    cuts = start_copies(
        [(w.at[my_rows], qkv.at[:, pl.ds(i * cols, cols)]) for i, w in enumerate((w_q, w_k, w_v))]
        + [(w.at[:, my_lanes], ffn.at[pl.ds(i * thin, thin)]) for i, w in enumerate((w_up, w_down))]
        + [(w_out.at[my_rows], ffn.at[pl.ds(2 * thin, slim)])],
        cut_sem,
    )
    signal_all([across, beside, partner, up, down])
    wait_copies(cuts)

    slot = lambda h, t, d: q_all.at[h, t, share, d]
    own = start_copies([(qkv, slot(half, turn, deep)), (ffn, f_deep.at[deep])], own_sem)

    def to_up(d):
        return remote(slot(half, turn, d), slot(half, turn, d), z_send.at[0, d], z_recv.at[d], up)

    def to_down(d):
        return remote(slot(half, turn, d), slot(half, turn, d), z_send.at[1, d], z_recv.at[d], down)

    third = f_deep.shape[1] // THIRDS

    def f_copies(d, side, device):
        return [
            remote(
                f_deep.at[d, pl.ds(i * third, third)], f_deep.at[d, pl.ds(i * third, third)],
                f_send.at[side, d, i], f_recv.at[d, i], device,
            )
            for i in range(THIRDS)
        ]

    f_up = lambda d: f_copies(d, 0, up)
    f_down = lambda d: f_copies(d, 1, down)

    def to_across(t, d):
        return remote(slot(half, t, d), slot(half, t, d), h_send.at[t, d], h_recv.at[t, d], across)

    def from_across(t, d):
        other = slot((half + 1) % 2, t, d)
        return remote(other, other, h_send.at[t, d], h_recv.at[t, d], across)

    def to_beside(d):
        return remote(slot(half, turn, d), slot(half, turn, d), t_send.at[d], t_recv.at[d], beside)

    def from_beside(d):
        other = slot(half, (turn + 1) % 2, d)
        return remote(other, other, t_send.at[d], t_recv.at[d], beside)

    def to_partner(t, d):
        piece = slot((share + 1) % 2, t, d)
        return remote(piece, piece, c_send.at[t, d], c_recv.at[t, d], partner)

    def from_partner(t, d):
        piece = q_all.at[share, t, (share + 1) % 2, d]
        return remote(piece, piece, c_send.at[t, d], c_recv.at[t, d], partner)

    cut = x_out.shape[1] // CUTS
    piece_rows = lambda i: pl.ds(i * cut, cut)
    x_next = [
        remote(
            hidden.at[half * 2 + (turn + 1) % 2, piece_rows(i)], x_out.at[0, piece_rows(i)],
            x_send.at[0, i], x_recv.at[0, i], beside,
        )
        for i in range(CUTS)
    ]
    x_mine = remote(
        hidden.at[half * 2 + turn], x_out.at[1], x_send.at[1, 0], x_recv.at[1, 0], partner
    )
    x_relay = [
        remote(
            x_out.at[0, piece_rows(i)], x_out.at[2, piece_rows(i)],
            x_send.at[2, i], x_recv.at[2, i], partner,
        )
        for i in range(CUTS)
    ]
    biases = [
        remote(src, dst, b_sem.at[0, i], b_sem.at[1, i], across)
        for i, (src, dst) in enumerate(((bias_q, far_q), (bias_v, far_v), (bias_u, far_u)))
    ]
    wait_copies(own)
    own_turn = (share + 1) % 2 == half

    def spread_own(d):
        to_across(turn, d).start()
        to_beside(d).start()

        @pl.when(own_turn)
        def _():
            to_partner(turn, d).start()

    def when(condition, *copies):
        @pl.when(condition)
        def _():
            for copy in copies:
                copy.start()

    when(deep < depth - 1, to_up(deep))
    when(deep > 0, to_down(deep))
    when(deep < depth - 1, f_up(deep)[0])
    when(deep > 0, f_down(deep)[0])
    spread_own(deep)
    x_next[0].start()
    for copy in biases:
        copy.start()
    x_mine.start()
    for k in range(1, depth):
        low, high = (deep + depth - k) % depth, (deep + k) % depth

        @pl.when(deep >= k)
        def _():
            to_up(low).wait_recv()
            when(deep < depth - 1, to_up(low))
            spread_own(low)

        @pl.when(deep + k < depth)
        def _():
            to_down(high).wait_recv()
            when(deep > 0, to_down(high))
            spread_own(high)

        if k < THIRDS:
            when(deep < depth - 1, f_up(deep)[k])
            when(deep > 0, f_down(deep)[k])
        x_next[k].start()

    for i in range(depth, THIRDS):
        when(deep < depth - 1, f_up(deep)[i])
        when(deep > 0, f_down(deep)[i])
    for copy in x_next[depth:]:
        copy.start()
    for k in range(depth):
        d = (deep + k) % depth
        from_beside(d).wait_recv()
        to_across((turn + 1) % 2, d).start()

        @pl.when(own_turn)
        def _():
            to_partner((turn + 1) % 2, d).start()

    f_side = [
        remote(
            f_deep.at[deep, pl.ds(i * third, third)], home.at[deep, pl.ds(i * third, third)],
            n_send.at[j, i], n_recv.at[j, i], device,
        )
        for i in range(THIRDS)
        for j, (home, device) in enumerate(((n1, beside), (n2, across)))
    ]
    for copy in f_side:
        copy.start()

    def f_step(k):
        low, high = (deep + depth - k) % depth, (deep + k) % depth

        @pl.when(deep >= k)
        def _():
            for copy in f_up(low):
                copy.wait_recv()
                when(deep < depth - 1, copy)

        @pl.when(deep + k < depth)
        def _():
            for copy in f_down(high):
                copy.wait_recv()
                when(deep > 0, copy)

    def x_step(step):
        for i in range(step * CUTS // (depth + 1), (step + 1) * CUTS // (depth + 1)):
            x_next[i].wait_recv()
            x_relay[i].start()

    f_step(1)
    for step, t in enumerate((turn, (turn + 1) % 2)):
        for k in range(depth):
            d = (deep + k) % depth
            from_across(t, d).wait_recv()

            @pl.when(jnp.logical_not(own_turn))
            def _():
                to_partner(t, d).start()

        x_step(step)
        if step == 0 and depth > 2:
            f_step(2)
    for k in range(3, depth):
        x_step(k - 1)
        f_step(k)
    for step in range(max(2, depth - 1), depth + 1):
        x_step(step)

    for t in range(2):
        for d in range(depth):
            from_partner(t, d).wait_recv()
    x_mine.wait_recv()
    for copy in x_relay + biases + f_side:
        copy.wait_recv()
    for d in range(depth):
        for copy in (to_across(0, d), to_across(1, d), to_beside(d), to_partner(0, d), to_partner(1, d)):
            copy.wait_send()

        @pl.when(jnp.logical_and(deep < depth - 1, deep >= d))
        def _():
            for copy in [to_up(d)] + f_up(d):
                copy.wait_send()

        @pl.when(jnp.logical_and(deep > 0, deep <= d))
        def _():
            for copy in [to_down(d)] + f_down(d):
                copy.wait_send()

    for copy in x_next + x_relay + [x_mine] + biases + f_side:
        copy.wait_send()


def fetch(hidden_in, weights, biases, depth):
    span, width = hidden_in.shape[1:]
    thin, cols = weights[0].shape
    slim = thin // 4
    bf16, shape = jnp.bfloat16, jax.ShapeDtypeStruct
    pair = DMA((2, depth))
    return pl.pallas_call(
        fetch_kernel,
        out_shape=(
            shape((3, span, width), bf16),
            shape((2, 2, 2, depth, slim, 3 * cols), bf16),
            *(shape((depth, 2 * thin + slim, cols), bf16) for _ in range(3)),
            *(shape(b.shape, bf16) for b in biases),
        ),
        in_specs=[ANY_SPEC] * 7 + [VMEM_SPEC] * 3,
        out_specs=(ANY_SPEC, VMEM_SPEC) + (ANY_SPEC,) * 3 + (VMEM_SPEC,) * 3,
        scratch_shapes=[
            pltpu.VMEM((slim, 3 * cols), bf16), pltpu.VMEM((2 * thin + slim, cols), bf16),
            DMA((6,)), DMA((2,)), DMA((3, CUTS)), DMA((3, CUTS)), pair, DMA((depth,)),
            DMA((2, depth, THIRDS)), DMA((depth, THIRDS)),
            pair, pair, DMA((depth,)), DMA((depth,)), pair, pair, DMA((2, 3)),
            DMA((2, THIRDS)), DMA((2, THIRDS)),
        ],
        compiler_params=pltpu.CompilerParams(
            vmem_limit_bytes=63 * 1024 * 1024, collective_id=0, has_side_effects=True
        ),
        cost_estimate=pl.CostEstimate(
            flops=30 * 10**9, bytes_accessed=10 * 10**6, transcendentals=0
        ),
        name="fetch",
    )(hidden_in, *weights, *biases)


SUBS = 4


def settle_kernel(
    parts_depth, hidden, x_in, dqkv, w_qkv, g_first, front_sums, rear_sums, up_sums, head_sums,
    *rest,
):
    f32, bf16 = jnp.float32, jnp.bfloat16
    parts, corners = rest[:3], rest[3 : 3 + parts_depth]
    (
        out, qkv_out, f_out, small_out,
        x_v, d_v, w_v, first_v, part_v, small_v, small_got,
        back_v, got_v, fin_v, land_v, tot_v, zf_v, ff_v,
        corner_v, corner_out, corner_in, grad_v, swap_v, pq_v, yl_v, xs_v, xl_v, rs_v, zq_v, qf_v,
        in_sem, out_sem, send_sem, recv_sem,
    ) = rest[3 + parts_depth :]
    half, turn, share = my_spot()
    deep = lax.axis_index("dp")
    depth = tot_v.shape[0]
    span = hidden.shape[1]
    sub = span // SUBS
    other = (share + 1) % 2
    far_half, far_turn = (half + 1) % 2, (turn + 1) % 2
    across, beside, partner = neighbours()
    deeps = [{"dp": (deep + k) % depth} for k in range(1, depth)]
    ids = iter(range(send_sem.shape[0]))
    started = []

    def link(src, dst, device):
        i = next(ids)
        copy = remote(src, dst, send_sem.at[i], recv_sem.at[i], device)
        started.append(copy)
        return copy

    def go(src, dst, device):
        copy = link(src, dst, device)
        copy.start()
        return copy

    chunk = lambda i: pl.ds(i * span, span)
    chunks = [hidden.at[half * 2 + turn]] + [x_in.at[i] for i in range(3)]
    loads = [
        pltpu.make_async_copy(src, dst, in_sem.at[i])
        for i, (src, dst) in enumerate(
            [(w_qkv, w_v)]
            + [(dqkv.at[chunk(i)], d_v.at[chunk(i)]) for i in (2, 3, 0, 1)]
            + [(p, part_v.at[i]) for i, p in enumerate(parts)]
            + [(g_first, first_v)]
            + [(c, x_v.at[chunk(i)]) for i, c in enumerate(chunks)]
        )
    ]
    corner_loads = start_copies(
        [(c, corner_v.at[i]) for i, c in enumerate(corners)], out_sem
    )
    for copy in loads:
        copy.start()
    diagonal = {"tensor": far_half, "context": far_turn * 2 + share}
    signal_all([across, beside, partner, diagonal] + deeps)
    wait_copies(corner_loads)
    corner_out[...] = sum(
        [corner_v[i].astype(f32) for i in range(1, depth)], corner_v[0].astype(f32)
    ).astype(bf16)
    corner = go(corner_out, corner_in, diagonal)
    small_v[...] = jnp.zeros_like(small_v)
    cols = up_sums.shape[1] // 2
    for g, (where, at) in enumerate(group_homes()):
        row = pl.ds(where * 2 + at // 2, 1)
        lanes = pl.ds(pl.multiple_of((at % 2) * cols, PAIR), cols)
        small_v[row, lanes] = up_sums[g // 2 : g // 2 + 1, (g % 2) * cols : (g % 2 + 1) * cols]
    small_v[4:7, :] = rear_sums[0:3, :]
    small_v[7:10, :] = front_sums[3:6, :]
    lane = lax.broadcasted_iota(jnp.int32, (1, small_v.shape[1]), 1)
    stats = jnp.where(lane == 5, front_sums[11:12, :], 0.0)
    for i in range(5):
        stats = jnp.where(lane == i, jnp.sum(front_sums[6 + i : 7 + i, :], 1, keepdims=True), stats)
    small_v[10:11, :] = stats
    small_v[11:13, :] = head_sums[0:2, :]

    s0 = go(small_v, small_got.at[0], partner)
    wait_copies(loads[:5] + loads[8:9])
    outs = []
    first_id = next(ids)
    next(ids)

    def give(i):
        return remote(
            back_v.at[i], got_v.at[i], send_sem.at[first_id + i], recv_sem.at[first_id + i], partner
        )

    rows = lambda j: pl.ds(j * sub, sub)

    def put(ref, h, t):
        copy = pltpu.make_async_copy(ref, out.at[h * 2 + t], out_sem.at[len(outs)])
        copy.start()
        outs.append(copy)

    own_put = pltpu.make_async_copy(fin_v.at[0], out.at[half * 2 + turn], out_sem.at[0])
    outs.append(own_put)
    x_subs = [link(fin_v.at[0, rows(j)], land_v.at[1, rows(j)], across) for j in range(SUBS)]
    y_subs = [link(fin_v.at[1, rows(j)], land_v.at[0, rows(j)], beside) for j in range(SUBS // 2)]

    def back_step(i, carry):
        at = pl.ds(pl.multiple_of((i + 2) % 4 * span, span), span)
        value = dot_nt(d_v[at, :], w_v[...])

        @pl.when(i < 2)
        def _():
            back_v[i] = value.astype(bf16)
            give(i).start()

        @pl.when(i >= 2)
        def _():
            give(i - 2).wait_recv()
            whole_sum = value + first_v[at, :] + got_v[i - 2].astype(f32)
            fin_v[i - 2] = whole_sum.astype(bf16)

        @pl.when(i == 2)
        def _():
            for copy in x_subs + [own_put]:
                copy.start()

        @pl.when(i == 3)
        def _():
            for copy in y_subs:
                copy.start()

        return carry

    lax.fori_loop(0, 4, back_step, 0)
    started += [give(0), give(1)]
    wait_copies(loads[5:8])
    tot_v[...] = (
        part_v[0].astype(f32) + part_v[1].astype(f32) + part_v[2].astype(f32)
    ).astype(bf16)
    z_f = [
        go(tot_v.at[(deep + k + 1) % depth], zf_v.at[k], device) for k, device in enumerate(deeps)
    ]


    s0.wait_recv()
    s0.wait_send()
    small_v[...] += small_got[0]
    s1 = go(small_v, small_got.at[1], beside)
    wait_copies(loads[9:])
    third = grad_v.shape[0] // 3

    def grad_step(i, carry):
        at = pl.ds(pl.multiple_of(i * third, PAIR), third)
        grad_v[at, :] = dot_tn(x_v[:, at], d_v[...]).astype(bf16)
        return carry

    lax.fori_loop(0, 3, grad_step, 0)
    slim = swap_v.shape[2]

    def grad_rows(d, t, s):
        return grad_v[pl.ds(pl.multiple_of((d * 4 + t * 2 + s) * slim, 16), slim), :]

    for d in range(depth):
        for t in range(2):
            swap_v[d, t] = grad_rows(d, t, other)
    swap = go(swap_v, pq_v.at[share], partner)
    for d in range(depth):
        for t in range(2):
            pq_v[share, d, t] = grad_rows(d, t, share)
    s1.wait_recv()
    s1.wait_send()
    small_v[...] += small_got[1]
    s2 = go(small_v, small_got.at[2], across)
    swap.wait_recv()
    keep_v = lambda h, t: pq_v[h, :, t]
    q1 = go(pq_v.at[far_half, :, far_turn], yl_v.at[0], beside)
    q2 = go(pq_v.at[half, :, far_turn], yl_v.at[1], beside)
    y_subs += [
        go(fin_v.at[1, rows(j)], land_v.at[0, rows(j)], beside) for j in range(SUBS // 2, SUBS)
    ]
    s2.wait_recv()
    s2.wait_send()
    small_v[...] += small_got[2]
    s3 = [go(small_v, small_got.at[3 + k], device) for k, device in enumerate(deeps)]
    relays = []

    def relay(j):
        y_subs[j].wait_recv()
        relays.append(go(land_v.at[0, rows(j)], land_v.at[2, rows(j)], across))

    for j in range(SUBS // 2):
        relay(j)
    q1.wait_recv()
    xs_v[...] = (keep_v(far_half, turn).astype(f32) + yl_v[0].astype(f32)).astype(bf16)
    qx = go(xs_v, xl_v, across)

    for copy in z_f:
        copy.wait_recv()
    ranks = range(depth - 1)
    spread = lambda ref, got: sum([got[k].astype(f32) for k in ranks], ref[deep].astype(f32))
    corner.wait_recv()
    ff_v[turn, share] = (spread(tot_v, zf_v) + corner_in[...].astype(f32)).astype(bf16)

    def gather_first(ref):
        piece = ref.at[turn, share]
        return go(piece, piece, beside), go(piece, piece, partner)

    def gather_next(ref, first):
        first.wait_recv()
        piece = ref.at[far_turn, share]
        return go(piece, piece, partner)

    f_first = gather_first(ff_v)
    q2.wait_recv()
    for j in range(SUBS // 2, SUBS):
        relay(j)
    qx.wait_recv()
    rs_v[...] = (
        keep_v(half, turn).astype(f32) + yl_v[1].astype(f32) + xl_v[...].astype(f32)
    ).astype(bf16)
    z_q = [
        go(rs_v.at[(deep + k + 1) % depth], zq_v.at[k], device) for k, device in enumerate(deeps)
    ]
    for copy in s3:
        copy.wait_recv()
    small_out[...] = small_v[...] + sum([small_got[4 + k] for k in range(depth - 2)], small_got[3])
    f_next = gather_next(ff_v, f_first[0])
    for copy in z_q:
        copy.wait_recv()
    qf_v[turn, share] = spread(rs_v, zq_v).astype(bf16)
    q_first = gather_first(qf_v)
    put(land_v.at[0], half, far_turn)
    for copy in x_subs:
        copy.wait_recv()
    put(land_v.at[1], far_half, turn)
    f_first[1].wait_recv()
    f_next.wait_recv()
    ends = start_copies([(ff_v, f_out)], in_sem)
    q_next = gather_next(qf_v, q_first[0])
    for copy in relays:
        copy.wait_recv()
    put(land_v.at[2], far_half, far_turn)
    q_first[1].wait_recv()
    q_next.wait_recv()
    last = pltpu.make_async_copy(qf_v, qkv_out, in_sem.at[2])
    last.start()
    wait_copies(ends + [last] + outs)
    waited = [s0, s1, s2]
    for copy in started:
        if not any(copy is w for w in waited):
            copy.wait_send()


def settle(hidden_in, x_in, dqkv, w_qkv, g_first, sums, parts, corners):
    rows, width = g_first.shape
    span = hidden_in.shape[1]
    depth, tall, cols = parts[0].shape
    wide = dqkv.shape[1]
    slim = width // depth // 4
    f32, bf16, shape = jnp.float32, jnp.bfloat16, jax.ShapeDtypeStruct
    v = pltpu.VMEM
    count = 80
    return pl.pallas_call(
        functools.partial(settle_kernel, depth),
        out_shape=(
            shape((4, span, width), bf16), shape((2, 2, slim, wide), bf16),
            shape((2, 2, tall, cols), bf16), shape((16, width), f32),
        ),
        in_specs=[ANY_SPEC] * 5 + [VMEM_SPEC] * 4 + [ANY_SPEC] * (3 + depth),
        out_specs=(ANY_SPEC,) * 3 + (VMEM_SPEC,),
        scratch_shapes=[
            v((2 * rows, width), bf16), v((2 * rows, wide), bf16), v((width, wide), bf16),
            v((rows, width), f32), v((3, depth, tall, cols), bf16), v((16, width), f32),
            v((2 + depth, 16, width), f32),
            v((2, span, width), bf16), v((2, span, width), bf16), v((2, span, width), bf16),
            v((3, span, width), bf16),
            v((depth, tall, cols), bf16), v((depth - 1, tall, cols), bf16),
            v((2, 2, tall, cols), bf16),
            v((depth, tall, cols), bf16), v((tall, cols), bf16), v((tall, cols), bf16),
            v((width, wide), bf16), v((depth, 2, slim, wide), bf16),
            v((2, depth, 2, slim, wide), bf16), v((2, depth, slim, wide), bf16),
            v((depth, slim, wide), bf16), v((depth, slim, wide), bf16),
            v((depth, slim, wide), bf16), v((depth - 1, slim, wide), bf16),
            v((2, 2, slim, wide), bf16),
            DMA((20,)), DMA((max(4, depth),)), DMA((count,)), DMA((count,)),
        ],
        compiler_params=pltpu.CompilerParams(
            vmem_limit_bytes=63 * 1024 * 1024, collective_id=1, has_side_effects=True
        ),
        cost_estimate=pl.CostEstimate(
            flops=60 * 10**9, bytes_accessed=30 * 10**6, transcendentals=0
        ),
        name="settle",
    )(hidden_in, x_in, dqkv, w_qkv, g_first, *sums, *parts, *corners)


def finish_kernel(
    grad, qkv, ffn, small,
    grad_home, o_q, o_bq, o_k, o_v, o_bv, o_o, o_bo, o_g1, o_s1, o_up, o_bup, o_down, o_bdown,
    o_g2, o_s2, o_rms,
    grad_in, grad_out, in_sem, out_sem,
):
    f32 = jnp.float32
    seqs, span, width = grad.shape
    half = my_spot()[0]
    thin = o_q.shape[0]
    cols = o_q.shape[1]
    loads = start_copies([(grad.at[i], grad_in.at[i]) for i in range(seqs)], in_sem)
    stores = []
    for i in range(seqs):
        loads[i].wait()
        grad_out[i] = grad_in[i].astype(f32)
        stores.append(pltpu.make_async_copy(grad_out.at[i], grad_home.at[i], out_sem.at[i]))
        stores[i].start()
    for i, ref in enumerate((o_q, o_k, o_v)):
        ref[...] = qkv[:, i * cols : (i + 1) * cols].astype(f32)
    slim = ffn.shape[1] - 2 * thin
    for p in range(4):
        at = slice(p * cols, (p + 1) * cols)
        o_up[:, at] = ffn[p, :thin, :].astype(f32)
        o_down[:, at] = ffn[p, thin : 2 * thin, :].astype(f32)
        o_o[p * slim : (p + 1) * slim, :] = ffn[p, 2 * thin :, :].astype(f32)
    flat = lambda row: row.reshape(row.shape[1])
    up = [small[pl.ds(half * 2 + i, 1), :] for i in range(2)]
    o_bup[...] = flat(jnp.concatenate(up, 1))
    for i, ref in enumerate((o_bo, o_g1, o_s1, o_bdown, o_g2, o_s2)):
        ref[...] = flat(small[4 + i : 5 + i, :])
    own = pl.ds(pl.multiple_of(half * cols, PAIR), cols)
    o_bq[...] = flat(small[11:12, own])
    o_bv[...] = flat(small[12:13, own])
    stats = small[10:11, :]
    o_rms[...] = jnp.sqrt(stats / (jnp.maximum(stats[:, 5:6], 1.0) * width))[:, :PAIR]
    wait_copies(stores)


def finish_all(grad, qkv, ffn, small):
    seqs, span, width = grad.shape
    thin, cols = qkv.shape[0], qkv.shape[1] // 3
    f32 = jnp.float32
    shape = lambda *s: jax.ShapeDtypeStruct(s, f32)
    outs = pl.pallas_call(
        finish_kernel,
        out_shape=(
            shape(seqs, span, width),
            shape(thin, cols), shape(cols), shape(thin, cols),
            shape(thin, cols), shape(cols), shape(thin, cols), shape(width), shape(width),
            shape(width), shape(thin, 4 * cols), shape(4 * cols), shape(thin, 4 * cols),
            shape(width), shape(width), shape(width), shape(1, PAIR),
        ),
        in_specs=[ANY_SPEC] + [VMEM_SPEC] * 3,
        out_specs=(ANY_SPEC,) + (VMEM_SPEC,) * 16,
        scratch_shapes=[
            pltpu.VMEM((seqs, span, width), grad.dtype), pltpu.VMEM((seqs, span, width), f32),
            DMA((seqs,)), DMA((seqs,)),
        ],
        compiler_params=WIDE_ROOM,
        name="finish_all",
    )(grad, qkv, ffn, small)
    outs = list(outs)
    outs[6], outs[12] = outs[6].T, outs[12].T
    return (*outs[:-1], outs[-1][0, :5])


def layer_norm(values, norm_gain, norm_shift):
    row_mean = jnp.mean(values, -1, keepdims=True)
    centered = values - row_mean
    row_var = jnp.mean(centered * centered, -1, keepdims=True)
    return centered * lax.rsqrt(row_var + EPSILON) * norm_gain + norm_shift


def gelu_tanh(values):
    return jax.nn.gelu(values, approximate=True)


def block_tables(random_seq, all_blocks, place):
    block = jnp.arange(2, all_blocks, dtype=jnp.int32)
    last = all_blocks - 1
    zero = jnp.zeros_like(block)
    true_ids = jnp.stack(
        [block, block - 1, block, jnp.minimum(block + 1, last), zero, zero + 1], -1
    )
    true_ids = jnp.concatenate([true_ids, random_seq[2:]], -1)
    flags = jnp.stack([block >= 3, block <= last - 1], -1).astype(jnp.int32)
    return (
        jnp.concatenate([place(true_ids), flags], -1).astype(jnp.int32),
        place(jnp.arange(2, dtype=jnp.int32)),
    )


def local(
    hidden_in, out_grad, segment_ids, token_valid, random_blocks,
    query_weight, query_bias, key_weight, value_weight, value_bias,
    output_weight, output_bias, norm1_gain, norm1_shift,
    up_weight, up_bias, down_weight, down_bias, norm2_gain, norm2_shift,
):
    f32, bf16 = jnp.float32, jnp.bfloat16
    seqs, span, width = hidden_in.shape
    length = segment_ids.shape[1]
    places = length // span
    halves = lax.axis_size("tensor")
    depth = lax.axis_size("dp")
    turns = seqs // halves
    shares = places // turns
    my_half = lax.axis_index("tensor")
    my_place = lax.axis_index("context")
    my_depth = lax.axis_index("dp")
    my_turn, my_share = my_place // shares, my_place % shares
    my_seq = my_half * turns + my_turn
    blocks = length // BLK
    rows = turns * span
    spots = [(h, t) for h in range(halves) for t in range(turns)]

    def send(value, half=0, turn=0, share=0):
        if half % halves == 0 and turn % turns == 0 and share % shares == 0:
            return value
        pairs = []
        for h in range(halves):
            for t in range(turns):
                for s in range(shares):
                    to_place = (t + turn) % turns * shares + (s + share) % shares
                    pairs.append(
                        ((t * shares + s) * halves + h, to_place * halves + (h + half) % halves)
                    )
        return lax.ppermute(value, ("context", "tensor"), pairs)

    def send_deep(value, step):
        return lax.ppermute(value, "dp", [(i, (i + step) % depth) for i in range(depth)])

    def pick(value, index, axis=0):
        return lax.dynamic_index_in_dim(value, index, axis, keepdims=False)

    def own_slice(value, count, which, axis):
        size = value.shape[axis] // count
        return lax.dynamic_slice_in_dim(value, which * size, size, axis)

    def gather_deep(value):
        if depth > 4:
            return lax.all_gather(value, "dp", axis=0)
        got = [value] + [send_deep(value, k) for k in range(1, depth)]
        ring = jnp.stack([got[depth - 1 - i % depth] for i in range(2 * depth - 1)])
        return lax.dynamic_slice_in_dim(ring, depth - 1 - my_depth, depth, 0)

    def reduce_deep(value):
        if depth > 4:
            return lax.psum_scatter(value, "dp", scatter_dimension=0)
        total = pick(value, my_depth).astype(f32)
        for k in range(1, depth):
            total = total + send_deep(pick(value, (my_depth + k) % depth), k).astype(f32)
        return total.astype(bf16)

    def gather_square(value):
        near = {spot: send(value, *spot) for spot in spots}
        near = jnp.stack([near[spot] for spot in spots])
        return [near] + [send(near, 0, 0, s) for s in range(1, shares)]

    def reduce_square(value):
        total = value[0].astype(f32)
        for i, (h, t) in enumerate(spots[1:], 1):
            total = total + send(value[i], -h, -t).astype(f32)
        return total.astype(bf16)

    def gather_places(value):
        near = [send(value, 0, t) for t in range(turns)]
        near = jnp.stack(near)
        far = jnp.stack([near] + [send(near, 0, 0, s) for s in range(1, shares)])
        return jnp.stack(
            [
                pick(pick(far, (my_share - s) % shares), (my_turn - t) % turns)
                for t in range(turns)
                for s in range(shares)
            ]
        )

    def sum_all(value):
        for step in range(halves.bit_length() - 1):
            value = value + send(value, 1 << step)
        size = 1
        while size < places:
            value = value + lax.ppermute(value, "context", [(i, i ^ size) for i in range(places)])
            size *= 2
        size = 1
        while size < depth:
            value = value + lax.ppermute(value, "dp", [(i, i ^ size) for i in range(depth)])
            size *= 2
        return value

    def bring(value):
        return jnp.concatenate(
            [
                send(pick(value, my_half * turns + (my_turn + k) % turns), 0, k)
                for k in range(turns)
            ],
            0,
        )

    def deliver(value):
        value = value.reshape(turns, span, width)
        got = jnp.stack([send(value[t], h, -t) for h, t in spots])
        return jnp.stack(
            [
                pick(got, (my_half - h) % halves * turns + (t - my_turn) % turns)
                for h in range(halves)
                for t in range(turns)
            ]
        )

    def after(value, *earlier):
        return lax.optimization_barrier((value, *earlier))[0]

    per = span // BLK

    def place(block_ids):
        chunk = block_ids // per
        turn, share = chunk // shares, chunk % shares
        spot = ((my_share - share) % shares) * turns + (my_turn - turn) % turns
        return spot * per + block_ids % per

    def in_order(row):
        return jnp.concatenate(
            [
                lax.dynamic_slice_in_dim(
                    row,
                    (((my_turn - k) % turns) * shares + (my_share - s) % shares) * span,
                    span,
                )
                for s in range(shares)
                for k in range(turns)
            ]
        )

    half_width = query_weight.shape[1]
    thin = query_weight.shape[0]
    slim = thin // places
    hidden = up_weight.shape[1] // places
    biases = jnp.concatenate([query_bias, value_bias, up_bias])

    def split_biases(by_half):
        by_half = jnp.stack([pick(by_half, (my_half - h) % halves) for h in range(halves)])
        return (
            by_half[:, at : at + b.shape[0]].reshape(-1)
            for b, at in ((query_bias, 0), (value_bias, half_width), (up_bias, 2 * half_width))
        )

    def spread(value, which, count):
        return lax.dynamic_update_slice_in_dim(
            jnp.zeros((value.shape[0] * count,), value.dtype), value, which * value.shape[0], 0
        )

    def small_rows(up_sums, group_at, norm_sums, stats):
        up_natural = jnp.zeros_like(up_sums)
        for i, at in enumerate(group_at):
            up_natural = lax.dynamic_update_slice_in_dim(
                up_natural, up_sums[i * hidden : (i + 1) * hidden], at * hidden, 0
            )
        stats = jnp.pad(stats, (0, width - stats.shape[0]))
        return jnp.concatenate(
            [up_natural.reshape(-1, width), *(row[None] for row in norm_sums), stats[None]], 0
        )

    def finish(layer_out, input_grad, qkv_shard, up_part, down_part, out_part, small):
        deep = up_weight.shape[1] * halves // width
        s_up, (s_o, s_g1, s_s1, s_down, s_g2, s_s2, stats, s_q, s_v) = (
            small[:deep].reshape(-1), small[deep : deep + 9]
        )
        s_q, s_v, s_up = (own_slice(value, halves, my_half, 0) for value in (s_q, s_v, s_up))
        input_rms = jnp.sqrt(stats[:5] / (jnp.maximum(stats[5], 1.0) * width))
        join = lambda w: jnp.moveaxis(w, 0, 1).reshape(thin, -1).astype(f32)
        shard_o = out_part.reshape(thin, -1)[:, :half_width].astype(f32).T
        shard_q, shard_k, shard_v = (qkv_shard[:, i].astype(f32) for i in range(3))
        return (
            layer_out, input_grad, shard_q, s_q, shard_k, shard_v, s_v, shard_o, s_o,
            s_g1, s_s1, join(up_part), s_up, join(down_part).T, s_down, s_g2, s_s2, input_rms,
        )

    if (turns, shares, halves) == (2, 2, 2) and depth <= 4 and rows % TILE == 0:
        near_b = [query_bias, value_bias, up_bias]
        x_in, q_all, f_deep, n1, n2, *far_b = fetch(
            hidden_in,
            [query_weight, key_weight, value_weight, up_weight, down_weight.T, output_weight.T],
            near_b, depth,
        )
        random = place(pick(random_blocks, my_seq)).reshape(-1)
        (
            att0, att1, q, k, v, lse, w_qkv, groups, key_code, query_code
        ) = project_attend(
            random, hidden_in, x_in, q_all, f_deep, n1, n2, segment_ids, token_valid,
            near_b[0], near_b[1], far_b[0], far_b[1],
        )
        vectors = [output_bias, norm1_gain, norm1_shift, down_bias, norm2_gain, norm2_shift]
        out0, out1, slope, g_second, unit, norm_t, downs, inverse, front_sums = ffn_front(
            att0, att1, hidden_in, x_in, out_grad, groups,
            key_code.reshape(length, PAIR), vectors, near_b[2], far_b[2],
        )
        g_first, do_own, do_far, layer_out, kept, turned, crossed, *corners, rear_sums, up_sums = ffn_rear(
            att0, att1, slope, g_second, unit, norm_t, out0, out1, downs, groups, inverse,
            norm1_gain,
        )
        parts = [kept, send(turned, 0, 1), send(crossed, 1)]
        corners = [send_deep(c, i) if i else c for i, c in enumerate(corners)]
        dqkv, layer_out, head_sums = attend_grad(
            random, do_own, do_far, q, k, v, layer_out, key_code, query_code, lse
        )
        dqkv, head_sums, parts, corners = lax.optimization_barrier(
            (dqkv, head_sums, parts, corners)
        )
        input_grad, qkv_shard, ffn_shard, small = settle(
            hidden_in, x_in, dqkv, w_qkv, g_first, (front_sums, rear_sums, up_sums, head_sums), parts,
            corners,
        )
        return (
            layer_out,
            *finish_all(
                input_grad, qkv_shard.reshape(thin, -1),
                ffn_shard.reshape((places,) + ffn_shard.shape[2:]), small,
            ),
        )

    seg = in_order(pick(segment_ids, my_seq))
    live = in_order(pick(token_valid, my_seq))
    random_seq = pick(random_blocks, my_seq)
    table, wide = block_tables(random_seq, blocks, place)
    key_code = jnp.broadcast_to(jnp.where(live == 1, seg, -1)[:, None], (length, PAIR))
    query_code = jnp.tile(seg.reshape(blocks, BLK), (1, PAIR // BLK))
    part = width // shares
    padded = -(-part // PAIR) * PAIR
    x_own = bring(hidden_in)
    qkv_piece = own_slice(
        jnp.concatenate([query_weight, key_weight, value_weight], 1), places, my_place, 0
    )
    qkv_all = jnp.stack(gather_square(gather_deep(qkv_piece)))
    per_half = shares // halves
    target = my_share // per_half
    qkv_all = jnp.stack(
        [
            pick(
                pick(qkv_all, (my_share - s) % shares),
                (my_half - target) % halves * turns + (my_turn - t) % turns,
            )
            for t in range(turns)
            for s in range(shares)
        ],
        1,
    ).reshape(width, 3, half_width)
    pad_cols = lambda w: jnp.pad(w, [(0, 0)] * (w.ndim - 1) + [(0, padded - part)])
    mine = lambda w: pad_cols(own_slice(w, per_half, my_share % per_half, w.ndim - 1))
    w_qkv = mine(qkv_all).reshape(width, 3 * padded)
    b_q, b_v, b_up = split_biases(jnp.stack([send(biases, h) for h in range(halves)]))
    mine_b = lambda b: pad_cols(own_slice(b, shares, my_share, 0))
    b_qkv = jnp.concatenate([mine_b(b_q), jnp.zeros((padded,), bf16), mine_b(b_v)]).astype(f32)

    ffn_piece = jnp.concatenate(
        [
            own_slice(up_weight, places, my_place, 1),
            own_slice(down_weight, places, my_place, 0).T,
            jnp.pad(
                own_slice(output_weight.T, places, my_place, 0),
                [(0, 0), (0, max(0, hidden - half_width))],
            ).reshape(-1, hidden),
        ],
        0,
    )
    ffn_all = gather_square(gather_deep(ffn_piece))
    groups = [
        (s, i, ffn_all[s][i]) for s in range(shares) for i in range(len(spots))
    ]
    w_up = jnp.concatenate([g[:, :thin].reshape(width, hidden) for _, _, g in groups], 1)
    w_down_t = jnp.concatenate(
        [g[:, thin : 2 * thin].reshape(width, hidden) for _, _, g in groups], 1
    )
    out_all = jnp.stack(
        [jnp.stack([g[:, 2 * thin :] for g in ffn_all[s]]) for s in range(shares)]
    )
    w_out_t = jnp.stack(
        [
            jnp.stack(
                [
                    pick(
                        pick(out_all, (my_share - s) % shares),
                        (my_half - h) % halves * turns + (my_turn - t) % turns,
                    )
                    for t in range(turns)
                    for s in range(shares)
                ],
                1,
            ).reshape(width, half_width)
            for h in range(halves)
        ],
        1,
    ).reshape(width, width)
    w_out_t = jnp.concatenate(
        [own_slice(w_out_t, shares, (my_share + k) % shares, 1) for k in range(shares)], 1
    )
    group_at = [
        ((my_half - spots[i][0]) % halves * places
         + (my_turn - spots[i][1]) % turns * shares + (my_share - s) % shares)
        for s, i, _ in groups
    ]
    b_up = jnp.concatenate(
        [lax.dynamic_slice_in_dim(b_up, at * hidden, hidden) for at in group_at]
    ).astype(f32)

    g_out = bring(out_grad).astype(f32)
    x_seq = jnp.concatenate([send(x_own, 0, 0, k) for k in range(shares)], 0)
    q, k, v = (
        (
            jnp.dot(x_seq, w_qkv[:, i * padded : (i + 1) * padded], preferred_element_type=f32)
            + b_qkv[i * padded : (i + 1) * padded]
        ).astype(bf16)
        for i in range(3)
    )
    att, lse = attend(table, wide, q, k, v, key_code, query_code)
    att = att[:, :part].reshape(shares, rows, part)
    att_own = jnp.concatenate([send(att[s], 0, 0, -s) for s in range(shares)], 1)
    attn_out = lax.dot_general(
        att_own, w_out_t, (((1,), (1,)), ((), ())), preferred_element_type=f32
    ) + output_bias.astype(f32)
    x_full = x_own.astype(f32)
    first_sum = x_full + attn_out
    gain_one, shift_one = norm1_gain.astype(f32), norm1_shift.astype(f32)
    normed = layer_norm(first_sum, gain_one, shift_one)
    normed_low = normed.astype(bf16)
    pre_act = jnp.dot(normed_low, w_up, preferred_element_type=f32) + b_up
    act_low = gelu_tanh(pre_act).astype(bf16)
    ffn_out = lax.dot_general(
        act_low, w_down_t, (((1,), (1,)), ((), ())), preferred_element_type=f32
    ) + down_bias.astype(f32)
    second_sum = normed + ffn_out
    gain_two, shift_two = norm2_gain.astype(f32), norm2_shift.astype(f32)
    layer_out, norm_back = jax.vjp(layer_norm, second_sum, gain_two, shift_two)
    g_second, gain_two_grad, shift_two_grad = norm_back(g_out)
    layer_out = deliver(layer_out.astype(bf16))
    g_ffn = g_second.astype(bf16)
    g_act = jnp.dot(g_ffn, w_down_t, preferred_element_type=f32)
    g_pre = jax.vjp(gelu_tanh, pre_act)[1](g_act)[0].astype(bf16)
    up_part = jnp.dot(normed_low.T, g_pre, preferred_element_type=f32).astype(bf16)
    down_part_t = jnp.dot(g_ffn.T, act_low, preferred_element_type=f32).astype(bf16)
    g_normed = g_second + jnp.dot(g_pre, w_up.T, preferred_element_type=f32)
    g_first, gain_one_grad, shift_one_grad = jax.vjp(layer_norm, first_sum, gain_one, shift_one)[1](
        g_normed
    )
    g_attn = g_first.astype(bf16)
    out_part_t = jnp.dot(g_attn.T, att_own, preferred_element_type=f32).astype(bf16)
    g_att = jnp.dot(g_attn, w_out_t, preferred_element_type=f32).astype(bf16)
    do = jnp.concatenate(
        [send(own_slice(g_att, shares, s, 1), 0, 0, s) for s in range(shares)], 0
    )
    dq, dk, dv = attend_back(table, wide, q, k, v, pad_cols(do), key_code, query_code, lse)

    out_natural = jnp.concatenate(
        [own_slice(out_part_t, shares, (s - my_share) % shares, 1) for s in range(shares)], 1
    ).reshape(depth, turns, shares, slim, halves, half_width)

    def ffn_group(s, i):
        h, t = spots[i]
        at = (s * len(spots) + i) * hidden
        out = pick(out_natural, (my_half - h) % halves, 4)
        out = pick(pick(out, (my_turn - t) % turns, 1), (my_share - s) % shares, 1)
        out = jnp.pad(out, [(0, 0), (0, 0), (0, max(0, hidden - half_width))])
        cut = lambda w: w[:, at : at + hidden].reshape(depth, thin, hidden)
        return jnp.concatenate(
            [cut(up_part), cut(down_part_t), out.reshape(depth, -1, hidden)], 1
        )

    ffn_grads = [
        jnp.stack([ffn_group(s, i) for i in range(len(spots))]) for s in range(shares)
    ]
    total = ffn_grads[0].astype(f32)
    for s in range(1, shares):
        total = total + send(ffn_grads[s], 0, 0, -s).astype(f32)
    ffn_shard = gather_places(reduce_deep(reduce_square(total.astype(bf16))))
    dqkv = jnp.concatenate([dq, dk, dv], 1)
    qkv_part = (
        jnp.dot(x_seq.T, dqkv, preferred_element_type=f32)
        .astype(bf16)
        .reshape(depth, turns, shares, slim, 3, padded)[..., :part]
    )
    got = jnp.stack(
        [send(pick(qkv_part, (my_share + s) % shares, 2), 0, 0, s) for s in range(shares)]
    )
    got = jnp.stack([pick(got, (my_share - s) % shares) for s in range(shares)], 4)
    got = got.reshape(depth, turns, slim, 3, halves, half_width)
    square = jnp.stack(
        [
            pick(pick(got, (my_half - h) % halves, 4), (my_turn - t) % turns, 1)
            for h, t in spots
        ]
    ).reshape(len(spots), depth, slim, 3 * half_width)
    qkv_shard = gather_places(reduce_deep(reduce_square(square))).reshape(thin, 3, half_width)
    back = jnp.dot(dqkv, w_qkv.T, preferred_element_type=f32).reshape(shares, rows, width)
    back_own = back[0]
    for s in range(1, shares):
        back_own = back_own + send(back[s].astype(bf16), 0, 0, -s).astype(f32)
    input_grad = deliver((g_first + back_own).astype(bf16)).astype(f32)

    sums = lambda value: jnp.sum(value.astype(f32), 0)
    valid = live[:rows].astype(f32)
    squares = lambda member: jnp.sum(valid * jnp.sum(member * member, -1))
    stats = jnp.stack(
        [squares(m) for m in (x_full, first_sum, second_sum, attn_out, ffn_out)]
        + [jnp.sum(valid), 0.0, 0.0]
    )
    up_sums = sums(g_pre)
    norm_sums = [
        sums(g_attn), gain_one_grad, shift_one_grad, sums(g_ffn), gain_two_grad, shift_two_grad
    ]
    small = small_rows(up_sums, group_at, norm_sums, stats)
    heads = [spread(sums(d)[:part], my_share, shares)[None] for d in (dq, dv)]
    small = sum_all(jnp.concatenate([small, *heads], 0))
    return finish(
        layer_out, input_grad, qkv_shard, ffn_shard[:, :thin], ffn_shard[:, thin : 2 * thin],
        ffn_shard[:, 2 * thin :], small,
    )


def solution(mesh):
    rows, plain = P("dp", "context", None), P()
    columns, across, halves = P("dp", "tensor"), P("tensor", "dp"), P("tensor")
    return jax.shard_map(
        local,
        mesh=mesh,
        in_specs=(
            rows, rows, P("dp", None), P("dp", None), P("dp", None, None),
            columns, halves, columns, columns, halves, across, plain, plain, plain,
            columns, halves, across, plain, plain, plain,
        ),
        out_specs=(
            rows, rows, columns, halves, columns, columns, halves, across, plain,
            plain, plain, columns, halves, across, plain, plain, plain, plain,
        ),
        check_vma=False,
    )
```

profile of v0, /device:TPU:0, one launch (start us, length us, event | category | flops | bytes accessed | tf_op | source)
XLA Modules:
  0.0 312.8 jit_solution(5736422047142299290)
XLA Ops:
  0.7 0.0 copy-start
  0.7 0.7 copy-done
  1.4 0.1 copy.41
  1.5 0.1 squeeze.7
  1.6 0.5 fusion.1.random
  2.1 45.4 %fetch.1 = (bf16[3,512,768]{2,1,0:T(8,128)(2,1)}, bf16[2,2,2,4,48,1152]{5,4,3,2,1,0:T(8,128)(2,1)}, bf16[4,432,384]{2,1,0:T(8,128)(2,1)}, bf16[4,432,384]{2,1,0:...) custom-call(bf16[4,512,768]{2,1,0:T(8,128)(2,1)} %hidden.7, ...), custom_call_target="tpu_custom_call" | custom-call | flops 30000001024 | bytes 10000000 | tf_op jit(solution)/shard_map/fetch/pallas_call | solution.py:1379
  47.5 44.0 %project_attend.1 = (bf16[1024,384]{1,0:T(8,128)(2,1)}, bf16[1024,384]{1,0:T(8,128)(2,1)}, bf16[2048,384]{1,0:T(8,128)(2,1)}, bf16[32,64,384]{2,1,0:T(8,128)(2,1...) custom-call(s32[96]{0:T(128)} %fusion.1.random, ...), custom_call_target="tpu_custom_call", output_to_operand_aliasing={{6}: (5, {}), {7}: (6, {})} | custom-call | flops 52344913920 | bytes 12582912 | tf_op jit(solution)/shard_map/project_attend/pallas_call | solution.py:569
  91.5 40.8 %ffn_front.1 = (bf16[512,768]{1,0:T(8,128)(2,1)}, bf16[512,768]{1,0:T(8,128)(2,1)}, bf16[4,1024,768]{2,1,0:T(8,128)(2,1)}, f32[1024,768]{1,0:T(8,128)}, f32[1024...) custom-call(bf16[1024,384]{1,0:T(8,128)(2,1)} %get-tuple-element.104, ...), custom_call_target="tpu_custom_call" | custom-call | flops 38000001024 | bytes 40000000 | tf_op jit(solution)/shard_map/ffn_front/pallas_call | solution.py:865
  132.3 43.3 %ffn_rear.1 = (f32[1024,768]{1,0:T(8,128)}, bf16[1024,384]{1,0:T(8,128)(2,1)}, bf16[1024,384]{1,0:T(8,128)(2,1)}, bf16[4,512,768]{2,1,0:T(8,128)(2,1)}, bf16[4,4...) custom-call(bf16[1024,384]{1,0:T(8,128)(2,1)} %get-tuple-element.104, ...), custom_call_target="tpu_custom_call" | custom-call | flops 44999999488 | bytes 40000000 | tf_op jit(solution)/shard_map/ffn_rear/pallas_call | solution.py:1088
  175.6 3.2 %collective-permute-start.2 = (bf16[432,384]{1,0:T(8,128)(2,1)}, bf16[432,384]{1,0:T(8,128)(2,1)S(1)}, u32[]{:S(2)}, u32[]{:S(2)}) collective-permute-start(bf16[432,384]{1,0:T(8,128)(2,1)} %get-tuple-element.138), channel_id=1, source_target_pairs={{0,8},{8,16},{16,24},{24,0},{1,9},{9,17},{17,25},{25,1},{2,10},{10... | collective-permute-start | bytes 995336 | tf_op jit(solution)/shard_map/ppermute | solution.py:1827
  178.8 1.4 collective-permute-start.3
  180.2 1.0 collective-permute-start.4
  181.2 1.1 collective-permute-start
  182.3 1.5 collective-permute-start.1
  183.8 50.4 %attend_grad.1 = (bf16[2048,1152]{1,0:T(8,128)(2,1)}, bf16[4,512,768]{2,1,0:T(8,128)(2,1)}, f32[8,768]{1,0:T(8,128)}) custom-call(s32[96]{0:T(128)} %fusion.1.random, bf16[1024,384]{1,0:T(8,128)(2,1)} %get-tuple-element.123.do0, bf16[1024,384]{1,0:T(8,128)(2,1)} %get-tuple-element.124.do1, bf16[2048,384]{1,0:T(8,128)(2,1)} %get-tuple-element.125.q_in, ...), custom_call_target="tpu_custom_call" | custom-call | flops 60397977600 | bytes 23592960 | tf_op jit(solution)/shard_map/attend_grad/pallas_call | solution.py:653
  234.2 0.0 collective-permute-done.2.rest_4_
  234.2 0.0 copy-start.2
  234.2 0.0 copy-start.3
  234.2 0.7 copy-done.2
  234.9 0.1 copy-done.3
  235.0 69.4 %settle.1 = (bf16[4,512,768]{2,1,0:T(8,128)(2,1)}, bf16[2,2,48,1152]{3,2,1,0:T(8,128)(2,1)}, bf16[2,2,432,384]{3,2,1,0:T(8,128)(2,1)}, f32[16,768]{1,0:T(8,128)}) custom-call(bf16[4,512,768]{2,1,0:T(8,128)(2,1)} %hidden.7, bf16[3,512,768]{2,1,0:T(8,128)(2,1)} %get-tuple-element.97.x_in, bf16[2048,1152]{1,0:T(8,128)(2,1)} %get-tuple-element.141.dqkv, ...), custom_call_target="tpu_custom_call" | custom-call | flops 60000002048 | bytes 30000000 | tf_op jit(solution)/shard_map/settle/pallas_call | solution.py:1663
  304.4 0.0 copy-start.1
  304.4 7.2 %finish_all.1 = (f32[4,512,768]{2,1,0:T(8,128)}, f32[192,384]{1,0:T(8,128)}, f32[384]{0:T(512)}, f32[192,384]{1,0:T(8,128)}, f32[192,384]{1,0:T(8,128)}, /*index...) custom-call(bf16[4,512,768]{2,1,0:T(8,128)(2,1)} %get-tuple-element., ...), custom_call_target="tpu_custom_call" | custom-call | tf_op jit(solution)/shard_map/finish_all/pallas_call | solution.py:1741
  311.6 1.1 slice_bitcast_fusion
  (6 shorter events, 0.0 us)
Async XLA Ops:
  0.7 0.7 copy-start
  175.6 58.6 %collective-permute-start.2 = (bf16[432,384]{1,0:T(8,128)(2,1)}, bf16[432,384]{1,0:T(8,128)(2,1)S(1)}, u32[]{:S(2)}, u32[]{:S(2)}) collective-permute-start(bf16[432,384]{1,0:T(8,128)(2,1)} %get-tuple-element.138), channel_id=1, source_target_pairs={{0,8},{8,16},{16,24},{24,0},{1,9},{9,17},{17,25},{25,1},{2,10},{10... | collective-permute-start | bytes 995336 | tf_op jit(solution)/shard_map/ppermute | solution.py:1827
  178.8 55.4 %collective-permute-start.3 = (bf16[432,384]{1,0:T(8,128)(2,1)}, bf16[432,384]{1,0:T(8,128)(2,1)S(1)}, u32[]{:S(2)}, u32[]{:S(2)}) collective-permute-start(bf16[432,384]{1,0:T(8,128)(2,1)} %get-tuple-element.139), channel_id=1, source_target_pairs={{0,16},{8,24},{16,0},{24,8},{1,17},{9,25},{17,1},{25,9},{2,18},{10... | collective-permute-start | bytes 995336 | tf_op jit(solution)/shard_map/ppermute | solution.py:1827
  180.2 54.0 %collective-permute-start.4 = (bf16[432,384]{1,0:T(8,128)(2,1)}, bf16[432,384]{1,0:T(8,128)(2,1)}, u32[]{:S(2)}, u32[]{:S(2)}) collective-permute-start(bf16[432,384]{1,0:T(8,128)(2,1)} %get-tuple-element.140), channel_id=1, source_target_pairs={{0,24},{8,0},{16,8},{24,16},{1,25},{9,1},{17,9},{25,17},{2,26},{10... | collective-permute-start | bytes 995336 | tf_op jit(solution)/shard_map/ppermute | solution.py:1827
  181.2 53.0 %collective-permute-start = (bf16[4,432,384]{2,1,0:T(8,128)(2,1)}, bf16[4,432,384]{2,1,0:T(8,128)(2,1)}, u32[]{:S(2)}, u32[]{:S(2)}) collective-permute-start(bf16[4,432,384]{2,1,0:T(8,128)(2,1)} %get-tuple-element.135), channel_id=1, source_target_pairs={{0,4},{2,6},{4,0},{6,2},{1,5},{3,7},{5,1},{7,3},{8,12},{10,14},{12... | collective-permute-start | bytes 3981320 | tf_op jit(solution)/shard_map/ppermute | solution.py:1824
  182.3 51.9 %collective-permute-start.1 = (bf16[4,432,384]{2,1,0:T(8,128)(2,1)}, bf16[4,432,384]{2,1,0:T(8,128)(2,1)}, u32[]{:S(2)}, u32[]{:S(2)}) collective-permute-start(bf16[4,432,384]{2,1,0:T(8,128)(2,1)} %get-tuple-element.136), channel_id=1, source_target_pairs={{0,1},{2,3},{4,5},{6,7},{1,0},{3,2},{5,4},{7,6},{8,9},{10,11},{12,... | collective-permute-start | bytes 3981320 | tf_op jit(solution)/shard_map/ppermute | solution.py:1824
  234.2 0.7 copy-start.2
  234.2 0.8 copy-start.3
  304.4 8.4 %copy-start.1 = (s32[4,32,3]{1,0,2:T(4,128)S(1)}, s32[4,32,3]{1,0,2:T(4,128)}, u32[]{:S(2)}) copy-start(s32[4,32,3]{1,0,2:T(4,128)} %param.24) | copy-start | bytes 4612
where the time goes:
time: 314 us; the launch traced here: 313 us
  Pallas kernels  300 us (96%)
  starting transfers between devices  8.19 us (3%)
    pallas_call x1, Pallas kernels, settle(): pl.pallas_call(functools.partial(settle_kernel, depth), out_shape=(shape(...  69.4 us
    pallas_call x1, Pallas kernels, attend_grad(): pl.pallas_call(attend_grad_kernel, out_shape=(shape((length, 3 * width),...  50.4 us
    pallas_call x1, Pallas kernels, fetch(): pl.pallas_call(fetch_kernel, out_shape=(shape((3, span, width), bf16), sh...  45.4 us
    pallas_call x1, Pallas kernels, project_attend(): pl.pallas_call(project_attend_kernel, out_shape=(shape((length // 2, widt...  44 us
    pallas_call x1, Pallas kernels, ffn_rear(): pl.pallas_call(ffn_rear_kernel, out_shape=(shape((rows, width), f32), sha...  43.3 us
    pallas_call x1, Pallas kernels, ffn_front(): pl.pallas_call(ffn_front_kernel, out_shape=(shape((rows // 2, width), bf1...  40.8 us
    pallas_call x1, Pallas kernels, finish_all(): pl.pallas_call(finish_kernel, out_shape=(shape(seqs, span, width), shape(...  7.24 us
  transfers between devices with their start and end apart: 5, of which 0 were waited for; matrix products, arithmetic and copies ran while one was open for 0% of the time, Pallas kernels for 16%

commit v1 on v0

--- a/solution.py
+++ b/solution.py
@@ -257,7 +257,7 @@
             )
 
         deltas = lax.fori_loop(
-            0, length // WIDE, first, (jnp.zeros((1, PAIR), jnp.float32),) * pairs
+            0, length // WIDE, first, (jnp.zeros((1, PAIR), jnp.float32),) * pairs, unroll=2
         )
         dq_acc[...] = jnp.zeros_like(dq_acc)
 
@@ -271,7 +271,7 @@
                 dq_acc[pair] += dot_tn(g_scores, keys)
             return carry
 
-        lax.fori_loop(0, length // WIDE, second, deltas)
+        lax.fori_loop(0, length // WIDE, second, deltas, unroll=2)
         for pair in range(pairs):
             lanes = slice(pair * PAIR, (pair + 1) * PAIR)
             both = dq_acc[pair]
@@ -1502,7 +1502,7 @@
     own_put = pltpu.make_async_copy(fin_v.at[0], out.at[half * 2 + turn], out_sem.at[0])
     outs.append(own_put)
     x_subs = [link(fin_v.at[0, rows(j)], land_v.at[1, rows(j)], across) for j in range(SUBS)]
-    y_subs = [link(fin_v.at[1, rows(j)], land_v.at[0, rows(j)], beside) for j in range(SUBS // 2)]
+    y_subs = [link(fin_v.at[1, rows(j)], land_v.at[0, rows(j)], beside) for j in range(SUBS - 1)]
 
     def back_step(i, carry):
         at = pl.ds(pl.multiple_of((i + 2) % 4 * span, span), span)
@@ -1576,7 +1576,7 @@
     q1 = go(pq_v.at[far_half, :, far_turn], yl_v.at[0], beside)
     q2 = go(pq_v.at[half, :, far_turn], yl_v.at[1], beside)
     y_subs += [
-        go(fin_v.at[1, rows(j)], land_v.at[0, rows(j)], beside) for j in range(SUBS // 2, SUBS)
+        go(fin_v.at[1, rows(j)], land_v.at[0, rows(j)], beside) for j in range(SUBS - 1, SUBS)
     ]
     s2.wait_recv()
     s2.wait_send()
@@ -1729,7 +1729,7 @@
     o_bq[...] = flat(small[11:12, own])
     o_bv[...] = flat(small[12:13, own])
     stats = small[10:11, :]
-    o_rms[...] = jnp.sqrt(stats / (jnp.maximum(stats[:, 5:6], 1.0) * width))[:, :PAIR]
+    o_rms[...] = flat(jnp.sqrt(stats / (jnp.maximum(stats[:, 5:6], 1.0) * width))[:, :5])
     wait_copies(stores)
 
 
@@ -1745,7 +1745,7 @@
             shape(thin, cols), shape(cols), shape(thin, cols),
             shape(thin, cols), shape(cols), shape(thin, cols), shape(width), shape(width),
             shape(width), shape(thin, 4 * cols), shape(4 * cols), shape(thin, 4 * cols),
-            shape(width), shape(width), shape(width), shape(1, PAIR),
+            shape(width), shape(width), shape(width), shape(5),
         ),
         in_specs=[ANY_SPEC] + [VMEM_SPEC] * 3,
         out_specs=(ANY_SPEC,) + (VMEM_SPEC,) * 16,
@@ -1758,7 +1758,7 @@
     )(grad, qkv, ffn, small)
     outs = list(outs)
     outs[6], outs[12] = outs[6].T, outs[12].T
-    return (*outs[:-1], outs[-1][0, :5])
+    return tuple(outs)
 
 
 def layer_norm(values, norm_gain, norm_shift):

time: 314 us -> 312 us (level)
  no operation moved by 1% of the time
where the time goes in v1:
time: 312 us; the launch traced here: 311 us
  Pallas kernels  299 us (96%)
  starting transfers between devices  8.19 us (3%)
    pallas_call x1, Pallas kernels, settle(): pl.pallas_call(functools.partial(settle_kernel, depth), out_shape=(shape(...  69.6 us
    pallas_call x1, Pallas kernels, attend_grad(): pl.pallas_call(attend_grad_kernel, out_shape=(shape((length, 3 * width),...  49.1 us
    pallas_call x1, Pallas kernels, fetch(): pl.pallas_call(fetch_kernel, out_shape=(shape((3, span, width), bf16), sh...  45.4 us
    pallas_call x1, Pallas kernels, project_attend(): pl.pallas_call(project_attend_kernel, out_shape=(shape((length // 2, widt...  44 us
    pallas_call x1, Pallas kernels, ffn_rear(): pl.pallas_call(ffn_rear_kernel, out_shape=(shape((rows, width), f32), sha...  43.3 us
    pallas_call x1, Pallas kernels, ffn_front(): pl.pallas_call(ffn_front_kernel, out_shape=(shape((rows // 2, width), bf1...  40.8 us
    pallas_call x1, Pallas kernels, finish_all(): pl.pallas_call(finish_kernel, out_shape=(shape(seqs, span, width), shape(...  7.24 us
  transfers between devices with their start and end apart: 5, of which 0 were waited for; matrix products, arithmetic and copies ran while one was open for 0% of the time, Pallas kernels for 16%

profile of v1, /device:TPU:0, one launch (start us, length us, event | category | flops | bytes accessed | tf_op | source)
XLA Modules:
  0.0 310.8 jit_solution(14024043494025007488)
XLA Ops:
  0.7 0.0 copy-start
  0.7 0.7 copy-done
  1.4 0.1 copy.41
  1.5 0.1 squeeze.4
  1.6 0.5 fusion.1.random
  2.1 45.4 %fetch.1 = (bf16[3,512,768]{2,1,0:T(8,128)(2,1)}, bf16[2,2,2,4,48,1152]{5,4,3,2,1,0:T(8,128)(2,1)}, bf16[4,432,384]{2,1,0:T(8,128)(2,1)}, bf16[4,432,384]{2,1,0:...) custom-call(bf16[4,512,768]{2,1,0:T(8,128)(2,1)} %hidden.7, ...), custom_call_target="tpu_custom_call" | custom-call | flops 30000001024 | bytes 10000000 | tf_op jit(solution)/shard_map/fetch/pallas_call | solution.py:1379
  47.5 44.0 %project_attend.1 = (bf16[1024,384]{1,0:T(8,128)(2,1)}, bf16[1024,384]{1,0:T(8,128)(2,1)}, bf16[2048,384]{1,0:T(8,128)(2,1)}, bf16[32,64,384]{2,1,0:T(8,128)(2,1...) custom-call(s32[96]{0:T(128)} %fusion.1.random, ...), custom_call_target="tpu_custom_call", output_to_operand_aliasing={{6}: (5, {}), {7}: (6, {})} | custom-call | flops 52344913920 | bytes 12582912 | tf_op jit(solution)/shard_map/project_attend/pallas_call | solution.py:569
  91.5 40.8 %ffn_front.1 = (bf16[512,768]{1,0:T(8,128)(2,1)}, bf16[512,768]{1,0:T(8,128)(2,1)}, bf16[4,1024,768]{2,1,0:T(8,128)(2,1)}, f32[1024,768]{1,0:T(8,128)}, f32[1024...) custom-call(bf16[1024,384]{1,0:T(8,128)(2,1)} %get-tuple-element.104, ...), custom_call_target="tpu_custom_call" | custom-call | flops 38000001024 | bytes 40000000 | tf_op jit(solution)/shard_map/ffn_front/pallas_call | solution.py:865
  132.3 43.3 %ffn_rear.1 = (f32[1024,768]{1,0:T(8,128)}, bf16[1024,384]{1,0:T(8,128)(2,1)}, bf16[1024,384]{1,0:T(8,128)(2,1)}, bf16[4,512,768]{2,1,0:T(8,128)(2,1)}, bf16[4,4...) custom-call(bf16[1024,384]{1,0:T(8,128)(2,1)} %get-tuple-element.104, ...), custom_call_target="tpu_custom_call" | custom-call | flops 44999999488 | bytes 40000000 | tf_op jit(solution)/shard_map/ffn_rear/pallas_call | solution.py:1088
  175.6 3.2 %collective-permute-start.2 = (bf16[432,384]{1,0:T(8,128)(2,1)}, bf16[432,384]{1,0:T(8,128)(2,1)S(1)}, u32[]{:S(2)}, u32[]{:S(2)}) collective-permute-start(bf16[432,384]{1,0:T(8,128)(2,1)} %get-tuple-element.138), channel_id=1, source_target_pairs={{0,8},{8,16},{16,24},{24,0},{1,9},{9,17},{17,25},{25,1},{2,10},{10... | collective-permute-start | bytes 995336 | tf_op jit(solution)/shard_map/ppermute | solution.py:1827
  178.8 1.4 collective-permute-start.3
  180.2 1.0 collective-permute-start.4
  181.2 1.1 collective-permute-start
  182.3 1.5 collective-permute-start.1
  183.8 49.1 %attend_grad.1 = (bf16[2048,1152]{1,0:T(8,128)(2,1)}, bf16[4,512,768]{2,1,0:T(8,128)(2,1)}, f32[8,768]{1,0:T(8,128)}) custom-call(s32[96]{0:T(128)} %fusion.1.random, bf16[1024,384]{1,0:T(8,128)(2,1)} %get-tuple-element.123.do0, bf16[1024,384]{1,0:T(8,128)(2,1)} %get-tuple-element.124.do1, bf16[2048,384]{1,0:T(8,128)(2,1)} %get-tuple-element.125.q_in, ...), custom_call_target="tpu_custom_call" | custom-call | flops 60397977600 | bytes 23592960 | tf_op jit(solution)/shard_map/attend_grad/pallas_call | solution.py:653
  232.9 0.0 collective-permute-done.2.rest_4_
  232.9 0.0 copy-start.2
  232.9 0.0 copy-start.3
  232.9 0.0 collective-permute-done.4.rest_6_
  232.9 0.7 copy-done.2
  233.6 0.1 copy-done.3
  233.7 69.6 %settle.1 = (bf16[4,512,768]{2,1,0:T(8,128)(2,1)}, bf16[2,2,48,1152]{3,2,1,0:T(8,128)(2,1)}, bf16[2,2,432,384]{3,2,1,0:T(8,128)(2,1)}, f32[16,768]{1,0:T(8,128)}) custom-call(bf16[4,512,768]{2,1,0:T(8,128)(2,1)} %hidden.7, bf16[3,512,768]{2,1,0:T(8,128)(2,1)} %get-tuple-element.97.x_in, bf16[2048,1152]{1,0:T(8,128)(2,1)} %get-tuple-element.141.dqkv, ...), custom_call_target="tpu_custom_call" | custom-call | flops 60000002048 | bytes 30000000 | tf_op jit(solution)/shard_map/settle/pallas_call | solution.py:1663
  303.4 0.0 copy-start.1
  303.4 7.2 %finish_all.1 = (f32[4,512,768]{2,1,0:T(8,128)}, f32[192,384]{1,0:T(8,128)}, f32[384]{0:T(512)}, f32[192,384]{1,0:T(8,128)}, f32[192,384]{1,0:T(8,128)}, /*index...) custom-call(bf16[4,512,768]{2,1,0:T(8,128)(2,1)} %get-tuple-element., ...), custom_call_target="tpu_custom_call" | custom-call | tf_op jit(solution)/shard_map/finish_all/pallas_call | solution.py:1741
  (5 shorter events, 0.0 us)
Async XLA Ops:
  0.7 0.7 copy-start
  175.6 57.3 %collective-permute-start.2 = (bf16[432,384]{1,0:T(8,128)(2,1)}, bf16[432,384]{1,0:T(8,128)(2,1)S(1)}, u32[]{:S(2)}, u32[]{:S(2)}) collective-permute-start(bf16[432,384]{1,0:T(8,128)(2,1)} %get-tuple-element.138), channel_id=1, source_target_pairs={{0,8},{8,16},{16,24},{24,0},{1,9},{9,17},{17,25},{25,1},{2,10},{10... | collective-permute-start | bytes 995336 | tf_op jit(solution)/shard_map/ppermute | solution.py:1827
  178.8 54.1 %collective-permute-start.3 = (bf16[432,384]{1,0:T(8,128)(2,1)}, bf16[432,384]{1,0:T(8,128)(2,1)S(1)}, u32[]{:S(2)}, u32[]{:S(2)}) collective-permute-start(bf16[432,384]{1,0:T(8,128)(2,1)} %get-tuple-element.139), channel_id=1, source_target_pairs={{0,16},{8,24},{16,0},{24,8},{1,17},{9,25},{17,1},{25,9},{2,18},{10... | collective-permute-start | bytes 995336 | tf_op jit(solution)/shard_map/ppermute | solution.py:1827
  180.2 52.7 %collective-permute-start.4 = (bf16[432,384]{1,0:T(8,128)(2,1)}, bf16[432,384]{1,0:T(8,128)(2,1)}, u32[]{:S(2)}, u32[]{:S(2)}) collective-permute-start(bf16[432,384]{1,0:T(8,128)(2,1)} %get-tuple-element.140), channel_id=1, source_target_pairs={{0,24},{8,0},{16,8},{24,16},{1,25},{9,1},{17,9},{25,17},{2,26},{10... | collective-permute-start | bytes 995336 | tf_op jit(solution)/shard_map/ppermute | solution.py:1827
  181.2 51.7 %collective-permute-start = (bf16[4,432,384]{2,1,0:T(8,128)(2,1)}, bf16[4,432,384]{2,1,0:T(8,128)(2,1)}, u32[]{:S(2)}, u32[]{:S(2)}) collective-permute-start(bf16[4,432,384]{2,1,0:T(8,128)(2,1)} %get-tuple-element.135), channel_id=1, source_target_pairs={{0,4},{2,6},{4,0},{6,2},{1,5},{3,7},{5,1},{7,3},{8,12},{10,14},{12... | collective-permute-start | bytes 3981320 | tf_op jit(solution)/shard_map/ppermute | solution.py:1824
  182.3 50.6 %collective-permute-start.1 = (bf16[4,432,384]{2,1,0:T(8,128)(2,1)}, bf16[4,432,384]{2,1,0:T(8,128)(2,1)}, u32[]{:S(2)}, u32[]{:S(2)}) collective-permute-start(bf16[4,432,384]{2,1,0:T(8,128)(2,1)} %get-tuple-element.136), channel_id=1, source_target_pairs={{0,1},{2,3},{4,5},{6,7},{1,0},{3,2},{5,4},{7,6},{8,9},{10,11},{12,... | collective-permute-start | bytes 3981320 | tf_op jit(solution)/shard_map/ppermute | solution.py:1824
  232.9 0.7 copy-start.2
  232.9 0.8 copy-start.3
  303.4 7.3 %copy-start.1 = (s32[4,32,3]{1,0,2:T(4,128)S(1)}, s32[4,32,3]{1,0,2:T(4,128)}, u32[]{:S(2)}) copy-start(s32[4,32,3]{1,0,2:T(4,128)} %param.24) | copy-start | bytes 4612
